TPU v7x, 256 devices: a whole 4x4x8 slice. The times are simulated.
256 devices in a mesh: row: 8 (over y, x_lo), col: 32 (over x_hi, z, core).
Axes of the slice: x: 4 (x_hi: 2, x_lo: 2; x = x_hi * 2 + x_lo), y: 4, z: 8, core: 2. Of those that a mesh axis runs over, the one named last changes fastest.
Arguments:
- inv_sep: bfloat16 [24576, 24576], P('row', 'col'), may hold values from -6 to 6
- lower_one: bfloat16 [24576, 256], P('col', 'row'), may hold values from -0.0390625 to 0.0390625
- upper_one: bfloat16 [256, 24576], P('col', 'row'), may hold values from -0.0390625 to 0.0390625
- diag_inv_one: float32 [256, 256], replicated, may hold values from -6 to 6
- blocks_one: int32 [160], replicated, may hold values from 0 to 191, as said below
- lower_two: bfloat16 [24576, 256], P('col', 'row'), may hold values from -0.046875 to 0.046875
- upper_two: bfloat16 [256, 24576], P('col', 'row'), may hold values from -0.046875 to 0.046875
- corner_lower: bfloat16 [256, 256], replicated, may hold values from -0.375 to 0.375
- corner_upper: bfloat16 [256, 256], replicated, may hold values from -0.375 to 0.375
- diag_inv_two: float32 [256, 256], replicated, may hold values from -6 to 6
- blocks_two: int32 [128], replicated, may hold values from 0 to 191, as said below
Outputs:
- inv_lower_one: bfloat16 [20480, 256], P(('row', 'col'))
- inv_upper_one: bfloat16 [256, 20480], P('row', 'col')
- inv_diag_one: float32 [256, 256], replicated
- inv_lower_two: bfloat16 [16384, 256], P(('row', 'col'))
- inv_upper_two: bfloat16 [256, 16384], P('row', 'col')
- inv_diag_two: float32 [256, 256], replicated
Inputs may be any that keep to these rules, and one draw needn't show every extreme that they name: `blocks_one`: distinct block indices in increasing order; each aligned run of 6 blocks holds exactly 5 of them; the first and the last block of the separator are listed. `blocks_two`: distinct block indices in increasing order, each of them also in blocks_one; each aligned run of 6 blocks holds exactly 4 of them; the first and the last block of the separator are listed.
All inputs are finite; a program needn't handle non-finite values.
Results may differ from a plain program's by a relative error of at most 0.0039.
Values may be sent and summed in bfloat16 or wider, within the bound.
A program may use at most 64 MiB of HBM per device.

v0:
```python
import jax
import jax.numpy as jnp
from jax import lax
from jax.sharding import PartitionSpec as P

B = 128


def highest(first_mat, second_mat):
    return jnp.dot(
        first_mat.astype(jnp.float32),
        second_mat.astype(jnp.float32),
        precision=lax.Precision.HIGHEST,
    )


def take_rows(matrix, blocks):
    shaped = matrix.reshape(matrix.shape[0] // B, B, matrix.shape[1])
    return jnp.take(shaped, blocks, axis=0).reshape(blocks.shape[0] * B, matrix.shape[1])


def take_cols(matrix, blocks):
    shaped = matrix.reshape(matrix.shape[0], matrix.shape[1] // B, B)
    return jnp.take(shaped, blocks, axis=1).reshape(matrix.shape[0], blocks.shape[0] * B)


def block_rows(blocks):
    return (blocks[:, None] * B + jnp.arange(B, dtype=jnp.int32)[None, :]).reshape(-1)


def places(wanted, listed):
    return jnp.sum((listed[None, :] < wanted[:, None]).astype(jnp.int32), axis=1)


def on_device(
    inv_sep,
    lower_one,
    upper_one,
    diag_inv_one,
    blocks_one,
    lower_two,
    upper_two,
    corner_lower,
    corner_upper,
    diag_inv_two,
    blocks_two,
):
    row_index = lax.axis_index("row")
    col_index = lax.axis_index("col")
    row_count = lax.axis_size("row")
    col_count = lax.axis_size("col")
    rows_here, cols_here = inv_sep.shape
    panel_width = diag_inv_one.shape[0]
    run_blocks = cols_here // B
    pick_one = blocks_one.shape[0] // col_count
    pick_two = blocks_two.shape[0] // col_count
    runs_group = col_count // row_count
    group_one = pick_one * runs_group
    group_two = pick_two * runs_group
    share_one = pick_one * B // row_count
    share_two = pick_two * B // row_count
    upper_rows = panel_width // row_count
    row_one = lax.dynamic_slice_in_dim(blocks_one, row_index * group_one, group_one) - row_index * (
        rows_here // B
    )
    row_two = lax.dynamic_slice_in_dim(blocks_two, row_index * group_two, group_two) - row_index * (
        rows_here // B
    )
    col_one = (
        lax.dynamic_slice_in_dim(blocks_one, col_index * pick_one, pick_one)
        - col_index * run_blocks
    )
    col_two = (
        lax.dynamic_slice_in_dim(blocks_two, col_index * pick_two, pick_two)
        - col_index * run_blocks
    )
    sep_one = take_cols(take_rows(inv_sep, row_one), col_one)
    sep_two = take_cols(take_rows(inv_sep, row_two), col_two)
    lower_spots = block_rows(places(row_two, row_one))
    upper_spots = places(col_two, col_one)
    corner_mine = lax.dynamic_slice_in_dim(corner_upper, row_index * upper_rows, upper_rows, 1)
    lower_p = lax.all_gather(take_rows(lower_one, col_one), "row", axis=1, tiled=True)
    upper_p = lax.all_gather(take_cols(upper_one, row_one), "col", axis=0, tiled=True)
    inv_lower_one = lax.psum_scatter(
        -jnp.dot(sep_one, lower_p, preferred_element_type=jnp.float32),
        "col",
        scatter_dimension=0,
        tiled=True,
    ).astype(jnp.bfloat16)
    inv_upper_one = lax.psum_scatter(
        -jnp.dot(upper_p, sep_one, preferred_element_type=jnp.float32),
        "row",
        scatter_dimension=0,
        tiled=True,
    ).astype(jnp.bfloat16)
    lower_c = lax.all_gather(take_rows(lower_two, col_two), "row", axis=1, tiled=True)
    upper_c = lax.all_gather(take_cols(upper_two, row_two), "col", axis=0, tiled=True)
    own_rows = col_index * share_one + jnp.arange(share_one, dtype=jnp.int32)
    chooser = (lower_spots[:, None] == own_rows[None, :]).astype(jnp.float32)
    carried = jnp.dot(inv_lower_one, corner_lower, preferred_element_type=jnp.float32)
    direct = jnp.dot(sep_two, lower_c, preferred_element_type=jnp.float32)
    shifted_part = jnp.dot(chooser, carried, precision=lax.Precision.HIGHEST)
    inv_lower_two = lax.psum_scatter(
        -(direct + shifted_part), "col", scatter_dimension=0, tiled=True
    ).astype(jnp.bfloat16)
    ancestor_cols = take_cols(inv_upper_one, upper_spots)
    direct = jnp.dot(upper_c, sep_two, preferred_element_type=jnp.float32)
    shifted_part = jnp.dot(corner_mine, ancestor_cols, preferred_element_type=jnp.float32)
    inv_upper_two = lax.psum_scatter(
        -(direct + shifted_part), "row", scatter_dimension=0, tiled=True
    ).astype(jnp.bfloat16)
    upper_slab = lax.dynamic_slice_in_dim(upper_p, col_index * share_one, share_one, 1)
    second_slab = lax.dynamic_slice_in_dim(upper_c, col_index * share_two, share_two, 1)
    first_part = jnp.dot(upper_slab, inv_lower_one, preferred_element_type=jnp.float32)
    cross = jnp.dot(ancestor_cols, lower_c, preferred_element_type=jnp.float32)
    second_part = jnp.dot(second_slab, inv_lower_two, preferred_element_type=jnp.float32) - highest(
        corner_mine, cross
    )
    first_total = lax.psum(first_part, ("row", "col"))
    inv_diag_one = diag_inv_one - first_total
    second_total = lax.psum(second_part, ("row", "col"))
    tail_term = highest(corner_upper, highest(inv_diag_one, corner_lower))
    inv_diag_two = diag_inv_two - (second_total - tail_term)
    return (inv_lower_one, inv_upper_one, inv_diag_one, inv_lower_two, inv_upper_two, inv_diag_two)


def solution(mesh):
    return jax.shard_map(
        on_device,
        mesh=mesh,
        in_specs=(
            P("row", "col"),
            P("col", "row"),
            P("col", "row"),
            P(),
            P(),
            P("col", "row"),
            P("col", "row"),
            P(),
            P(),
            P(),
            P(),
        ),
        out_specs=(
            P(("row", "col"), None),
            P("row", "col"),
            P(),
            P(("row", "col"), None),
            P("row", "col"),
            P(),
        ),
        check_vma=False,
    )
```

profile of v0, /device:TPU:1, one launch (start us, length us, event | category | flops | bytes accessed | tf_op | source)
XLA Modules:
  0.0 766.5 jit_solution(17721407719966944696)
XLA Ops:
  10.2 5.3 gather_fusion
  15.5 9.2 %reshape.206 = bf16[2560,6,128]{2,1,0:T(8,128)(2,1)} reshape(bf16[20,128,768]{2,1,0:T(8,128)(2,1)} %gather_fusion) | data formatting | bytes 7864320 | tf_op jit(solution)/shard_map/jit(_take)/gather | solution.py:19
  24.7 5.2 copy_select_fusion
  30.0 3.3 gather_fusion.1
  33.3 3.4 copy.41
  37.4 24.6 %all_gather.12 = bf16[640,256]{0,1:T(8,128)(2,1)S(1)} all-gather(bf16[640,32]{0,1:T(8,128)(2,1)S(1)} %bitcast_select_fusion.2), channel_id=1, replica_groups=mesh['row'=8,'col'=32] {'row'}, dimensions={1}, use_global_device_ids=true | all-gather | bytes 368640 | tf_op jit(solution)/shard_map/all_gather | solution.py:82
  62.0 2.3 bitcast_select_fusion
  64.3 2.8 convolution_negate_fusion
  67.2 26.7 %all-gather.3.cloned.1.call-done = bf16[256,2560]{1,0:T(8,128)(2,1)} async-done(((bf16[8,2560]{1,0:T(8,128)(2,1)}), bf16[256,2560]{1,0:T(8,128)(2,1)}) %all-gather.3.cloned.1.call-update) | async-done | bytes 1310736 | tf_op jit(solution)/shard_map/all_gather | solution.py:83
  93.9 3.4 convolution_negate_fusion.1
  98.8 3.1 gather_fusion.4
  102.1 4.6 reshape.207
  106.8 2.8 copy_select_fusion.1
  110.4 2.2 gather_fusion.5
  112.5 4.0 copy.46
  116.6 23.2 %all_gather.14 = bf16[512,256]{0,1:T(8,128)(2,1)S(1)} all-gather(bf16[512,32]{0,1:T(8,128)(2,1)S(1)} %bitcast_select_fusion.5), channel_id=1, replica_groups=mesh['row'=8,'col'=32] {'row'}, dimensions={1}, use_global_device_ids=true | all-gather | bytes 294912 | tf_op jit(solution)/shard_map/all_gather | solution.py:96
  143.8 66.8 %reduce-scatter.5.cloned.1.call-done = f32[80,256]{1,0:T(8,128)} async-done(((f32[2560,256]{1,0:T(8,128)}), f32[80,256]{1,0:T(8,128)}) %reduce-scatter.5.cloned.1.call-update) | async-done | bytes 81936 | tf_op jit(solution)/shard_map/reduce_scatter | solution.py:84
  211.6 3.5 fusion
  215.5 37.2 %reduce-scatter.7.cloned.1.call-done = f32[32,640]{1,0:T(8,128)} async-done(((f32[256,640]{1,0:T(8,128)}), f32[32,640]{1,0:T(8,128)}) %reduce-scatter.7.cloned.1.call-update) | async-done | bytes 81936 | tf_op jit(solution)/shard_map/reduce_scatter | solution.py:90
  254.5 83.5 %all-gather.5.cloned.1.call-done = bf16[256,2048]{1,0:T(8,128)(2,1)} async-done(((bf16[8,2048]{1,0:T(8,128)(2,1)}), bf16[256,2048]{1,0:T(8,128)(2,1)}) %all-gather.5.cloned.1.call-update) | async-done | bytes 1048592 | tf_op jit(solution)/shard_map/all_gather | solution.py:97
  338.0 2.8 fusion.1
  342.9 110.0 %reduce-scatter.9.cloned.1.call-done = f32[64,256]{1,0:T(8,128)} async-done(((f32[2048,256]{1,0:T(8,128)}), f32[64,256]{1,0:T(8,128)}) %reduce-scatter.9.cloned.1.call-update) | async-done | bytes 65552 | tf_op jit(solution)/shard_map/reduce_scatter | solution.py:103
  456.5 38.1 %reduce-scatter.11.cloned.1.call-done = f32[32,512]{1,0:T(8,128)} async-done(((f32[256,512]{1,0:T(8,128)}), f32[32,512]{1,0:T(8,128)}) %reduce-scatter.11.cloned.1.call-update) | async-done | bytes 65552 | tf_op jit(solution)/shard_map/reduce_scatter | solution.py:109
  496.1 260.3 %all-reduce.3.cloned.1.call-done = (f32[256,256]{1,0:T(8,128)}, f32[256,256]{1,0:T(8,128)}) async-done(((f32[256,256]{1,0:T(8,128)}, f32[256,256]{1,0:T(8,128)}), (f32[256,256]{1,0:T(8,128)}, f32[256,256]{1,0:T(8,128)})) %all-reduce.3.cloned.1.call-update) | async-done | bytes 524304 | tf_op jit(solution)/shard_map/psum | solution.py:119
  (92 shorter events, 23.7 us)
Async XLA Ops:
  7.2 247.0 %copy-start = (bf16[256,256]{1,0:T(8,128)(2,1)S(1)}, bf16[256,256]{1,0:T(8,128)(2,1)}, u32[]{:S(2)}) copy-start(bf16[256,256]{1,0:T(8,128)(2,1)} %param.19) | copy-start | bytes 393220
  7.2 86.7 %all-gather.3.cloned.1.call-start = ((), (), s32[]{:S(2)}) async-start(), calls=%async_computation.5 | async-start | bytes 1351680 | tf_op jit(solution)/shard_map/all_gather | solution.py:83
  10.1 200.5 %reduce-scatter.5.cloned.1.call-start = ((), (), s32[]{:S(2)}) async-start(), calls=%async_computation.4 | async-start | bytes 2703360 | tf_op jit(solution)/shard_map/reduce_scatter | solution.py:84
  24.7 5.2 copy-start.12
  33.3 3.4 copy-start.8
  67.1 30.3 %copy-start.11 = (s32[128]{0:T(128)S(1)}, s32[128]{0:T(128)}, u32[]{:S(2)}) copy-start(s32[128]{0:T(128)} %param.21) | copy-start | bytes 1540
  67.1 30.3 %copy-start.10 = (bf16[8,3072]{1,0:T(8,128)(2,1)S(1)}, bf16[8,3072]{1,0:T(8,128)(2,1)}, u32[]{:S(2)}) copy-start(bf16[8,3072]{1,0:T(8,128)(2,1)} %param.17) | copy-start | bytes 147460
  67.1 185.6 %reduce-scatter.7.cloned.1.call-start = ((), (), s32[]{:S(2)}) async-start(), calls=%async_computation.6 | async-start | bytes 737280 | tf_op jit(solution)/shard_map/reduce_scatter | solution.py:90
  97.3 240.7 %all-gather.5.cloned.1.call-start = ((), (), s32[]{:S(2)}) async-start(), calls=%async_computation.8 | async-start | bytes 1081344 | tf_op jit(solution)/shard_map/all_gather | solution.py:97
  98.8 354.1 %reduce-scatter.9.cloned.1.call-start = ((), (), s32[]{:S(2)}) async-start(), calls=%async_computation.7 | async-start | bytes 2162688 | tf_op jit(solution)/shard_map/reduce_scatter | solution.py:103
  106.8 3.0 copy-start.9
  141.7 69.8 %copy-start.2 = (bf16[256,256]{1,0:T(8,128)(2,1)S(1)}, bf16[256,256]{1,0:T(8,128)(2,1)}, u32[]{:S(2)}) copy-start(bf16[256,256]{1,0:T(8,128)(2,1)} %param.18) | copy-start | bytes 393220
  211.5 129.6 %copy-start.3 = (bf16[80,256]{1,0:T(8,128)(2,1)}, bf16[80,256]{1,0:T(8,128)(2,1)S(1)}, u32[]{:S(2)}) copy-start(bf16[80,256]{1,0:T(8,128)(2,1)S(1)} %convert_element_type.22) | copy-start | bytes 122884
  215.2 279.5 %reduce-scatter.11.cloned.1.call-start = ((), (), s32[]{:S(2)}) async-start(), calls=%async_computation.9 | async-start | bytes 589824 | tf_op jit(solution)/shard_map/reduce_scatter | solution.py:109
  254.4 201.4 %copy-start.4 = (f32[32,640]{1,0:T(8,128)S(1)}, f32[32,640]{1,0:T(8,128)}, u32[]{:S(2)}) copy-start(f32[32,640]{1,0:T(8,128)} %reduce-scatter.7.cloned.1.call-done) | copy-start | bytes 245764
  340.8 415.7 %copy-start.5 = (f32[256,256]{1,0:T(8,128)S(1)}, f32[256,256]{1,0:T(8,128)}, u32[]{:S(2)}) copy-start(f32[256,256]{1,0:T(8,128)} %param.14) | copy-start | bytes 786436
  340.8 416.9 %copy-start.6 = (f32[256,256]{1,0:T(8,128)S(1)}, f32[256,256]{1,0:T(8,128)}, u32[]{:S(2)}) copy-start(f32[256,256]{1,0:T(8,128)} %param.20) | copy-start | bytes 786436
  340.8 415.6 %all-reduce.3.cloned.1.call-start = ((), (), s32[]{:S(2)}) async-start(), calls=%async_computation.10 | async-start | bytes 1048576 | tf_op jit(solution)/shard_map/psum | solution.py:119
  453.7 306.0 %copy-start.7 = (bf16[64,256]{1,0:T(8,128)(2,1)}, bf16[64,256]{1,0:T(8,128)(2,1)S(1)}, u32[]{:S(2)}) copy-start(bf16[64,256]{1,0:T(8,128)(2,1)S(1)} %convert_element_type.25) | copy-start | bytes 98308
  757.4 2.3 copy-start.1
Sparse Core Ops, SparseCore 0:
  11.4 82.4 all-gather.2
  98.0 112.5 reduce-scatter.4
  213.3 39.3 reduce-scatter.6
  256.3 81.6 all-gather.4
  342.5 110.2 reduce-scatter.8
  455.2 39.3 reduce-scatter.10
  501.8 254.6 all-reduce.2
where the time goes:
time: 768 us; the launch traced here: 767 us
  waiting for transfers between devices  623 us (81%)
  blocking collectives  47.8 us (6%)
  local copies, waits for them, and re-layouts  39.2 us (5%)
  matrix products  21.4 us (3%)
  other arithmetic  20.7 us (3%)
  between operations  14.4 us (2%)
    psum x1, waiting for transfers between devices, on_device(): first_total = lax.psum(first_part, ('row', 'col'))  260 us
    reduce_scatter x1, waiting for transfers between devices, on_device(): lax.psum_scatter(-(direct + shifted_part), 'col', scatter_dimension=0, ti...  110 us
    all_gather x1, waiting for transfers between devices, on_device(): lax.all_gather(take_cols(upper_two, row_two), 'col', axis=0, tiled=True)  83.5 us
    reduce_scatter x1, waiting for transfers between devices, on_device(): lax.psum_scatter(-jnp.dot(sep_one, lower_p, preferred_element_type=jnp.fl...  66.8 us
    reduce_scatter x1, waiting for transfers between devices, on_device(): lax.psum_scatter(-(direct + shifted_part), 'row', scatter_dimension=0, ti...  38.1 us
    reduce_scatter x1, waiting for transfers between devices, on_device(): lax.psum_scatter(-jnp.dot(upper_p, sep_one, preferred_element_type=jnp.fl...  37.2 us
    all_gather x1, waiting for transfers between devices, on_device(): lax.all_gather(take_cols(upper_one, row_one), 'col', axis=0, tiled=True)  26.7 us
    all_gather x1, blocking collectives, on_device(): lax.all_gather(take_rows(lower_one, col_one), 'row', axis=1, tiled=True)  24.6 us
  transfers between devices with their start and end apart: 7, of which 7 were waited for; matrix products, arithmetic and copies ran while one was open for 10% of the time, Pallas kernels for 0%

commit v1 on v0

v1 whole, which is shorter than its diff:
```python
import functools

import jax
import jax.numpy as jnp
from jax import lax
from jax.experimental import pallas as pl
from jax.experimental.pallas import tpu as pltpu
from jax.sharding import PartitionSpec as P

B = 128
SPAN = 6
ONE = 5
TWO = 4
XH = 2
CORES = 2
MESH = pl.DeviceIdType.MESH
F32 = jnp.float32
BF16 = jnp.bfloat16


def mm(a, b):
    return jnp.dot(a, b, preferred_element_type=F32)


def exact(a, b):
    return jnp.dot(
        a, b, preferred_element_type=F32, precision=lax.Precision.HIGHEST
    )


def kernel(
    R,
    C,
    W,
    sel_any,
    sel2_any,
    own_u,
    own_x,
    pick_cols,
    cl_ref,
    cu_ref,
    dg1_ref,
    dg2_ref,
    l1_out,
    u1_out,
    d1_out,
    l2_out,
    u2_out,
    d2_out,
    sel,
    sel2,
    G,
    V,
    XG,
    X,
    Pm,
    cr,
    xs,
    xr,
    zs,
    zr,
    own,
    PU,
    PUb,
    ur_buf,
    dd,
    drc,
    dxs,
    drx,
    dz,
    Dall,
    tail,
    sem_sel,
    gz_s,
    gz_r,
    gx_s,
    gx_r,
    gc_s,
    gc_r,
    xg_s,
    xg_r,
    cs_s,
    cs_r,
    rx_s,
    rx_r,
    rz_s,
    rz_r,
    pu_s,
    pu_r,
    d_s,
    d_r,
    dz_s,
    dz_r,
    dr_s,
    dr_r,
):
    Z = C // (XH * CORES)
    runs = C // R
    nb1, nb2 = runs * ONE, runs * TWO
    ncol = ONE * B
    ur = W // C
    lw = W // R
    s1, s2 = ONE * B // R, TWO * B // R
    M = XH * Z
    uw = W // R

    r = lax.axis_index("row")
    c = lax.axis_index("col")
    k = lax.rem(c, CORES)
    z = lax.rem(c // CORES, Z)
    xh = c // (CORES * Z)

    def col_of(xh_, z_, k_):
        return (xh_ * Z + z_) * CORES + k_

    core_dev = (r, col_of(xh, z, 1 - k))
    x_dev = (r, col_of(1 - xh, z, k))

    def z_at(i):
        return lax.rem(z + 1 + i, Z)

    def r_at(i):
        return lax.rem(r + 1 + i, R)

    def z_dev(zz):
        return (r, col_of(xh, zz, k))

    def row_dev(rr):
        return (rr, c)

    def rcopy(src, dst, ssem, rsem, dev):
        return pltpu.make_async_remote_copy(
            src_ref=src,
            dst_ref=dst,
            send_sem=ssem,
            recv_sem=rsem,
            device_id=dev,
            device_id_type=MESH,
        )

    def loop(n, body):
        def step(i, carry):
            body(i)
            return carry

        lax.fori_loop(0, n, step, 0)

    sel_copy = pltpu.make_async_copy(sel_any, sel, sem_sel.at[0])
    sel2_copy = pltpu.make_async_copy(sel2_any, sel2, sem_sel.at[1])
    sel_copy.start()
    sel2_copy.start()

    barrier = pltpu.get_barrier_semaphore()
    pl.semaphore_signal(barrier, inc=1, device_id=core_dev, device_id_type=MESH)
    pl.semaphore_signal(barrier, inc=1, device_id=x_dev, device_id_type=MESH)

    def greet_z(i):
        pl.semaphore_signal(barrier, inc=1, device_id=z_dev(z_at(i)), device_id_type=MESH)

    def greet_r(i):
        pl.semaphore_signal(barrier, inc=1, device_id=row_dev(r_at(i)), device_id_type=MESH)

    loop(Z - 1, greet_z)
    loop(R - 1, greet_r)

    for half in range(2):
        G[half, c] = own_u[half]
        XG[half, r] = own_x[half]

    pl.semaphore_wait(barrier, 2 + (Z - 1) + (R - 1))

    def gz(src_z, to_z):
        slot = col_of(xh, src_z, k)
        return rcopy(G.at[:, slot], G.at[:, slot], gz_s.at[to_z], gz_r.at[src_z], z_dev(to_z))

    def gx(src_xh, src_z):
        slot = col_of(src_xh, src_z, k)
        return rcopy(G.at[:, slot], G.at[:, slot], gx_s.at[src_z], gx_r.at[src_z], x_dev)

    def gc(src_xh, src_z, src_k):
        slot = col_of(src_xh, src_z, src_k)
        sem = src_xh * Z + src_z
        return rcopy(G.at[:, slot], G.at[:, slot], gc_s.at[sem], gc_r.at[sem], core_dev)

    def xg(src_r, to_r):
        return rcopy(
            XG.at[:, src_r], XG.at[:, src_r], xg_s.at[to_r], xg_r.at[src_r], row_dev(to_r)
        )

    loop(R - 1, lambda i: xg(r, r_at(i)).start())
    loop(Z - 1, lambda i: gz(z, z_at(i)).start())
    gx(xh, z).start()
    gc(xh, z, k).start()

    loop(R - 1, lambda i: xg(r_at(i), r).wait_recv())
    x1t = XG[0].reshape(W, ncol)
    lct = XG[1].reshape(W, ncol)
    clt = cl_ref[...].astype(F32).T.astype(BF16)
    x2 = (lct.astype(F32) - mm(clt, x1t)).T
    x2hi = x2.astype(BF16)
    X[:, 0:W] = x1t.astype(F32).T.astype(BF16)
    X[:, W : 2 * W] = x2hi
    X[:, 2 * W : 3 * W] = (x2 - x2hi.astype(F32)).astype(BF16)

    def cs(m):
        return rcopy(Pm.at[m, 1 - k], cr.at[m], cs_s.at[m], cs_r.at[m], core_dev)

    sel_copy.wait()
    sel2_copy.wait()

    def lower(m):
        first = sel[pl.ds(pl.multiple_of(m * (2 * s1), 16), 2 * s1), :]
        p1 = mm(first, X[:, 0:W])
        Pm[m, 0, 0:s1, :] = p1[0:s1]
        Pm[m, 1, 0:s1, :] = p1[s1:]
        rows = sel2[pl.ds(pl.multiple_of(m * (2 * s2), 16), 2 * s2), :]
        p2 = mm(rows, X[:, W : 2 * W]) + mm(rows, X[:, 2 * W : 3 * W])
        Pm[m, 0, s1 : s1 + s2, :] = p2[0:s2]
        Pm[m, 1, s1 : s1 + s2, :] = p2[s2:]
        cs(m).start()

    loop(Z, lambda i: lower((1 - xh) * Z + z_at(i)))

    def pass_on(i):
        lower(xh * Z + z_at(i))

        @pl.when(i < Z - 1)
        def _():
            zz = z_at(i)
            gz(zz, z).wait_recv()
            gx(xh, zz).start()
            gc(xh, zz, k).start()

    loop(Z, pass_on)

    def rx(zz):
        return rcopy(xs.at[zz], xr.at[zz], rx_s.at[zz], rx_r.at[zz], x_dev)

    def rz(src_z, to_z):
        return rcopy(zs.at[to_z], zr.at[src_z], rz_s.at[to_z], rz_r.at[src_z], z_dev(to_z))

    def to_x(i):
        zz = z_at(i)
        m = (1 - xh) * Z + zz
        cs(m).wait_recv()
        xs[zz] = (Pm[m, k] + cr[m]).astype(BF16)
        rx(zz).start()

    loop(Z, to_x)

    def to_z(i):
        zz = z_at(i)
        m = xh * Z + zz
        cs(m).wait_recv()
        rx(zz).wait_recv()
        total = Pm[m, k] + cr[m] + xr[zz].astype(F32)

        @pl.when(i < Z - 1)
        def _():
            zs[zz] = total.astype(BF16)
            rz(z, zz).start()

        @pl.when(i == Z - 1)
        def _():
            own[...] = total

        zg = lax.rem(z + i, Z)
        gx(1 - xh, zg).wait_recv()
        gc(1 - xh, zg, k).start()

    loop(Z, to_z)

    def all_in(i):
        gc(i // Z, lax.rem(i, Z), 1 - k).wait_recv()

    loop(M, all_in)
    cu = cu_ref[...]
    wide = 2 * B if nb1 % 2 == 0 else B

    def second(j):
        at = pl.ds(pl.multiple_of(j * wide, wide), wide)
        up = G[0, :, :, at].reshape(W, wide)
        uc = G[1, :, :, at].reshape(W, wide)
        v = uc.astype(F32) - mm(cu, up)
        hi = v.astype(BF16)
        V[0, :, at] = up
        V[1, :, at] = hi
        V[2, :, at] = (v - hi.astype(F32)).astype(BF16)

    loop(nb1 * B // wide, second)

    def upper(j):
        PU[j] = mm(V[j], sel[...])

    loop(3, upper)
    PU[1] = PU[1] + PU[2]
    PUb[0] = PU[0].astype(BF16).reshape(R, uw, ncol)
    PUb[1] = PU[1].astype(BF16).reshape(R, uw, ncol)

    def pu(src_r, to_r):
        return rcopy(PUb.at[:, to_r], ur_buf.at[:, src_r], pu_s.at[to_r], pu_r.at[src_r], row_dev(to_r))

    loop(R - 1, lambda i: pu(r, r_at(i)).start())

    tail[...] = dg2_ref[...] + exact(
        cu.astype(F32), exact(dg1_ref[...], cl_ref[...].astype(F32))
    )

    def from_z(i):
        zz = z_at(i)
        rz(zz, z).wait_recv()
        own[...] = own[...] + zr[zz].astype(F32)

    loop(Z - 1, from_z)
    l1_out[...] = (-own[0:s1, :]).astype(BF16)
    l2_out[...] = (-own[s1 : s1 + s2, :]).astype(BF16)

    mine = pl.ds(pl.multiple_of(r * uw, 16), uw)

    def from_r(i):
        rr = r_at(i)
        pu(rr, r).wait_recv()
        PU[0, mine, :] = PU[0, mine, :] + ur_buf[0, rr].astype(F32)
        PU[1, mine, :] = PU[1, mine, :] + ur_buf[1, rr].astype(F32)

    loop(R - 1, from_r)
    u1 = (-PU[0, mine, :]).astype(BF16)
    u2 = (-PU[1, mine, :]).astype(BF16)
    dd[0] = mm(u1, X[:, 0:W])
    dd[1] = mm(u2, X[:, W : 2 * W]) + mm(u2, X[:, 2 * W : 3 * W])
    d_core = rcopy(dd.at[1 - k], drc, d_s.at[0], d_r.at[0], core_dev)
    d_core.start()
    u1_out[...] = u1
    u2_out[...] = mm(u2, pick_cols[...]).astype(BF16)

    d_core.wait_recv()
    dxs[...] = dd[k] + drc[...]
    d_x = rcopy(dxs, drx, d_s.at[1], d_r.at[1], x_dev)
    d_x.start()
    d_x.wait_recv()
    dz[z] = dxs[...] + drx[...]

    def dzc(src_z, to_z):
        return rcopy(dz.at[src_z], dz.at[src_z], dz_s.at[to_z], dz_r.at[src_z], z_dev(to_z))

    loop(Z - 1, lambda i: dzc(z, z_at(i)).start())
    loop(Z - 1, lambda i: dzc(z_at(i), z).wait_recv())
    total = dz[0]
    for i in range(1, Z):
        total = total + dz[i]
    Dall[k, r] = total

    def drow(src_r, to_r):
        return rcopy(
            Dall.at[k, src_r], Dall.at[k, src_r], dr_s.at[to_r], dr_r.at[src_r], row_dev(to_r)
        )

    loop(R - 1, lambda i: drow(r, r_at(i)).start())
    loop(R - 1, lambda i: drow(r_at(i), r).wait_recv())

    def d_both(src_k):
        return rcopy(Dall.at[src_k], Dall.at[src_k], d_s.at[2], d_r.at[2], core_dev)

    d_both(k).start()
    d_both(1 - k).wait_recv()
    d1_out[...] = dg1_ref[...] - Dall[0].reshape(W, W)
    d2_out[...] = tail[...] - Dall[1].reshape(W, W)

    def left_z(i):
        zz = z_at(i)
        gz(z, zz).wait_send()
        rz(z, zz).wait_send()
        dzc(z, zz).wait_send()

    def left_r(i):
        rr = r_at(i)
        xg(r, rr).wait_send()
        pu(r, rr).wait_send()
        drow(r, rr).wait_send()

    def left_x(i):
        gx(xh, i).wait_send()
        rx(i).wait_send()

    def left_c(i):
        gc(i // Z, lax.rem(i, Z), k).wait_send()
        cs(i).wait_send()

    loop(Z - 1, left_z)
    loop(R - 1, left_r)
    loop(Z, left_x)
    loop(M, left_c)
    d_core.wait_send()
    d_x.wait_send()
    d_both(k).wait_send()


def pick(
    R,
    C,
    one_ref,
    two_ref,
    sep,
    lp_ref,
    lc_ref,
    up_ref,
    uc_ref,
    sel,
    sel2,
    own_u,
    own_x,
    pick_cols,
):
    r = lax.axis_index("row")
    c = lax.axis_index("col")
    runs = C // R
    nb1 = runs * ONE
    ur = up_ref.shape[0]
    lw = lp_ref.shape[0]

    def one_at(run, s):
        return one_ref[run * ONE + s]

    def two_at(run, t):
        return two_ref[run * TWO + t]

    def in_two(run, b):
        hit = (two_at(run, 0) == b).astype(jnp.int32)
        for t in range(1, TWO):
            hit = hit + (two_at(run, t) == b).astype(jnp.int32)
        return hit

    col_at = [pl.multiple_of((one_at(c, s) - c * SPAN) * B, B) for s in range(ONE)]

    def row_at(b):
        return pl.multiple_of((b - r * (runs * SPAN)) * B, B)

    def some_run(q, carry):
        run = r * runs + q
        for s in range(ONE):
            b = one_at(run, s)
            at = row_at(b)
            to = pl.ds(pl.multiple_of((q * ONE + s) * B, B), B)
            for t in range(ONE):
                sel[to, t * B : (t + 1) * B] = sep[pl.ds(at, B), pl.ds(col_at[t], B)]
            own_u[0, :, to] = up_ref[:, pl.ds(at, B)]
            piece = uc_ref[:, pl.ds(at, B)].astype(F32)
            hit = jnp.full((ur, B), in_two(run, b))
            own_u[1, :, to] = jnp.where(hit > 0, piece, 0.0).astype(BF16)
        for t in range(TWO):
            at = row_at(two_at(run, t))
            to = pl.ds(pl.multiple_of((q * TWO + t) * B, B), B)
            for s in range(ONE):
                sel2[to, s * B : (s + 1) * B] = sep[pl.ds(at, B), pl.ds(col_at[s], B)]
        return carry

    lax.fori_loop(0, runs, some_run, 0)

    same = lax.broadcasted_iota(jnp.int32, (B, B), 0) == lax.broadcasted_iota(jnp.int32, (B, B), 1)
    eye = jnp.where(same, 1.0, 0.0)
    for s in range(ONE):
        b = one_at(c, s)
        to = pl.ds(s * B, B)
        own_x[0, :, to] = lp_ref[:, pl.ds(col_at[s], B)]
        piece = lc_ref[:, pl.ds(col_at[s], B)].astype(F32)
        hit = jnp.full((lw, B), in_two(c, b))
        own_x[1, :, to] = jnp.where(hit > 0, piece, 0.0).astype(BF16)
        for t in range(TWO):
            hit = jnp.full((B, B), (two_at(c, t) == b).astype(jnp.int32))
            pick_cols[to, t * B : (t + 1) * B] = jnp.where(hit > 0, eye, 0.0).astype(BF16)


def on_device(
    R,
    C,
    inv_sep,
    lower_one,
    upper_one,
    diag_inv_one,
    blocks_one,
    lower_two,
    upper_two,
    corner_lower,
    corner_upper,
    diag_inv_two,
    blocks_two,
):
    W = diag_inv_one.shape[0]
    Z = C // (XH * CORES)
    M = XH * Z
    runs = C // R
    nb1 = runs * ONE
    ncol = ONE * B
    ur, lw, uw = W // C, W // R, W // R
    s1, s2 = ONE * B // R, TWO * B // R
    sh = s1 + s2
    vmem = pl.BlockSpec(memory_space=pltpu.VMEM)
    smem = pl.BlockSpec(memory_space=pltpu.SMEM)
    dma = pltpu.SemaphoreType.DMA
    picked = pl.pallas_call(
        functools.partial(pick, R, C),
        out_shape=(
            jax.ShapeDtypeStruct((nb1 * B, ncol), BF16),
            jax.ShapeDtypeStruct((runs * TWO * B, ncol), BF16),
            jax.ShapeDtypeStruct((2, ur, nb1 * B), BF16),
            jax.ShapeDtypeStruct((2, lw, ncol), BF16),
            jax.ShapeDtypeStruct((ncol, TWO * B), BF16),
        ),
        in_specs=[smem, smem] + [vmem] * 5,
        out_specs=(vmem,) * 5,
        compiler_params=pltpu.CompilerParams(vmem_limit_bytes=24 * 2**20),
        name="pick",
    )(blocks_one, blocks_two, inv_sep, lower_one.T, lower_two.T, upper_one, upper_two)
    return pl.pallas_call(
        functools.partial(kernel, R, C, W),
        out_shape=(
            jax.ShapeDtypeStruct((s1, W), BF16),
            jax.ShapeDtypeStruct((uw, ncol), BF16),
            jax.ShapeDtypeStruct((W, W), F32),
            jax.ShapeDtypeStruct((s2, W), BF16),
            jax.ShapeDtypeStruct((uw, TWO * B), BF16),
            jax.ShapeDtypeStruct((W, W), F32),
        ),
        in_specs=[pl.BlockSpec(memory_space=pl.ANY)] * 2 + [vmem] * 7,
        out_specs=(vmem,) * 6,
        scratch_shapes=[
            pltpu.VMEM((nb1 * B, ncol), BF16),
            pltpu.VMEM((runs * TWO * B, ncol), BF16),
            pltpu.VMEM((2, C, ur, nb1 * B), BF16),
            pltpu.VMEM((3, W, nb1 * B), BF16),
            pltpu.VMEM((2, R, lw, ncol), BF16),
            pltpu.VMEM((ncol, 3 * W), BF16),
            pltpu.VMEM((M, 2, sh, W), F32),
            pltpu.VMEM((M, sh, W), F32),
            pltpu.VMEM((Z, sh, W), BF16),
            pltpu.VMEM((Z, sh, W), BF16),
            pltpu.VMEM((Z, sh, W), BF16),
            pltpu.VMEM((Z, sh, W), BF16),
            pltpu.VMEM((sh, W), F32),
            pltpu.VMEM((3, W, ncol), F32),
            pltpu.VMEM((2, R, uw, ncol), BF16),
            pltpu.VMEM((2, R, uw, ncol), BF16),
            pltpu.VMEM((2, uw, W), F32),
            pltpu.VMEM((uw, W), F32),
            pltpu.VMEM((uw, W), F32),
            pltpu.VMEM((uw, W), F32),
            pltpu.VMEM((Z, uw, W), F32),
            pltpu.VMEM((2, R, uw, W), F32),
            pltpu.VMEM((W, W), F32),
        ]
        + [dma((n,)) for n in (2, Z, Z, Z, Z, M, M, R, R, M, M, Z, Z, Z, Z, R, R, 3, 3, Z, Z, R, R)],
        compiler_params=pltpu.CompilerParams(
            collective_id=0, has_side_effects=True, vmem_limit_bytes=40 * 2**20
        ),
        name="panels",
    )(*picked, corner_lower, corner_upper, diag_inv_one, diag_inv_two)


def solution(mesh):
    R, C = mesh.shape["row"], mesh.shape["col"]
    return jax.shard_map(
        functools.partial(on_device, R, C),
        mesh=mesh,
        in_specs=(
            P("row", "col"),
            P("col", "row"),
            P("col", "row"),
            P(),
            P(),
            P("col", "row"),
            P("col", "row"),
            P(),
            P(),
            P(),
            P(),
        ),
        out_specs=(
            P(("row", "col"), None),
            P("row", "col"),
            P(),
            P(("row", "col"), None),
            P("row", "col"),
            P(),
        ),
        check_vma=False,
    )
```

time: 768 us -> 105 us (0.14)
  waiting for transfers between devices: 623 us -> 0 us
  Pallas kernels: 0 us -> 93 us
  blocking collectives: 47.8 us -> 0 us
  local copies, waits for them, and re-layouts: 39.2 us -> 10.7 us
  matrix products: 21.4 us -> 0 us
  other arithmetic: 20.7 us -> 0 us
  between operations: 14.4 us -> 0.71 us
    psum x1 -> x0, waiting for transfers between devices: 260 us -> none  [on_device(): first_total = lax.psum(first_part, ('row', 'col'))]
    reduce_scatter x4 -> x0, waiting for transfers between devices: 252 us -> none  [the longest x1 110 us: on_device(): lax.psum_scatter(-(direct + shifted_part), 'col', scatter_dimension=0, ti...]
    all_gather x2 -> x0, waiting for transfers between devices: 110 us -> none  [the longest x1 83.5 us: on_device(): lax.all_gather(take_cols(upper_two, row_two), 'col', axis=0, tiled=True)]
    pallas_call x0 -> x2, Pallas kernels: none -> 93 us  [the longest x1 90.7 us: on_device(): pl.pallas_call(functools.partial(kernel, R, C, W), out_shape=(jax.ShapeDt...]
    all_gather x2 -> x0, blocking collectives: 47.8 us -> none  [the longest x1 24.6 us: on_device(): lax.all_gather(take_rows(lower_one, col_one), 'row', axis=1, tiled=True)]
    gather x13 -> x0, local copies, waits for them, and re-layouts: 38.8 us -> none  [the longest x6 23.4 us: take_rows(): jnp.take(shaped, blocks, axis=0)]
    dot_general x13 -> x0, matrix products: 21.4 us -> none  [the longest x1 3.51 us: on_device(): shifted_part = jnp.dot(chooser, carried, precision=lax.Precision.HIGHEST)]
    select_n x13 -> x0, other arithmetic: 13.5 us -> none  [the longest x6 8.09 us: take_rows(): jnp.take(shaped, blocks, axis=0)]
  transfers between devices with their start and end apart: 7 -> 0, of which waited for: 7 -> 0; matrix products, arithmetic and copies ran while one was open for 10% -> 0% of each run, Pallas kernels for 0% -> 0%
where the time goes in v1:
time: 105 us; the launch traced here: 104 us
  Pallas kernels  93 us (89%)
  local copies, waits for them, and re-layouts  10.7 us (10%)
    pallas_call x1, Pallas kernels, on_device(): pl.pallas_call(functools.partial(kernel, R, C, W), out_shape=(jax.ShapeDt...  90.7 us
    unnamed x28, local copies, waits for them, and re-layouts  10.7 us
    pallas_call x1, Pallas kernels, on_device(): pl.pallas_call(functools.partial(pick, R, C), out_shape=(jax.ShapeDtypeSt...  2.32 us

profile of v1, /device:TPU:1, one launch (start us, length us, event | category | flops | bytes accessed | tf_op | source)
XLA Modules:
  0.0 104.4 jit_solution(7188645367940871535)
XLA Ops:
  0.6 0.0 copy-start
  0.6 2.3 %copy-done = bf16[3072,768]{1,0:T(8,128)(2,1)S(1)} copy-done((bf16[3072,768]{1,0:T(8,128)(2,1)S(1)}, bf16[3072,768]{1,0:T(8,128)(2,1)}, u32[]{:S(2)}) %copy-start) | copy-done | bytes 4718616
  3.0 0.0 copy-start.5
  3.0 0.8 copy-done.5
  3.8 0.0 copy-start.6
  3.8 0.8 copy-done.6
  4.6 0.0 copy-start.7
  4.6 0.8 copy-done.7
  5.4 0.0 copy-start.8
  5.4 0.8 copy-done.8
  6.2 0.7 copy-done.9
  6.9 0.7 copy-done.10
  7.5 2.3 %pick.1 = (bf16[2560,640]{1,0:T(8,128)(2,1)S(1)}, bf16[2048,640]{1,0:T(8,128)(2,1)S(1)}, bf16[2,8,2560]{2,1,0:T(8,128)(2,1)S(1)}, bf16[2,32,640]{2,1,0:T(8,128)(2,1)S(1)}, bf16[640,512]{1,0:T(8,128)(2,1)S(1)}) custom-call(s32[160]{0:T(256)S(1)} %copy-done.9, s32[128]{0:T(128)S(1)} %copy-done.10, bf16[3072,768]{1,0:T(8,128)(2,1)S(1)} %copy-done, ...), custom_call_target="tpu_custom_call" | custom-call | tf_op jit(solution)/shard_map/pick/pallas_call | solution.py:500
  9.8 0.0 copy-done.1
  9.9 0.0 copy-done.2
  9.9 0.0 copy-done.3
  9.9 0.0 copy-done.4
  9.9 90.7 %panels.1 = (bf16[80,256]{1,0:T(8,128)(2,1)S(1)}, bf16[32,640]{1,0:T(8,128)(2,1)S(1)}, f32[256,256]{1,0:T(8,128)S(1)}, bf16[64,256]{1,0:T(8,128)(2,1)S(1)}, bf16...) custom-call(bf16[2560,640]{1,0:T(8,128)(2,1)S(1)} %get-tuple-element.11.sel_any, ...), custom_call_target="tpu_custom_call" | custom-call | tf_op jit(solution)/shard_map/panels/pallas_call | solution.py:514
  100.6 0.6 copy.23
  101.2 0.6 copy.24
  101.8 0.7 copy.25
  102.5 0.6 copy.26
  103.1 0.6 copy.27
  103.7 0.7 copy.28
  (6 shorter events, 0.0 us)
Async XLA Ops:
  0.6 2.3 %copy-start = (bf16[3072,768]{1,0:T(8,128)(2,1)S(1)}, bf16[3072,768]{1,0:T(8,128)(2,1)}, u32[]{:S(2)}) copy-start(bf16[3072,768]{1,0:T(8,128)(2,1)} %sep.1) | copy-start | bytes 14155780
  3.0 0.8 copy-start.5
  3.8 0.8 copy-start.6
  4.6 0.8 copy-start.7
  5.4 0.8 copy-start.8
  6.2 0.7 copy-start.9
  6.8 0.7 copy-start.10
  7.5 2.3 %copy-start.1 = (f32[256,256]{1,0:T(8,128)S(1)}, f32[256,256]{1,0:T(8,128)}, u32[]{:S(2)}) copy-start(f32[256,256]{1,0:T(8,128)} %dg1_ref.1) | copy-start | bytes 786436
  7.5 2.4 %copy-start.2 = (f32[256,256]{1,0:T(8,128)S(1)}, f32[256,256]{1,0:T(8,128)}, u32[]{:S(2)}) copy-start(f32[256,256]{1,0:T(8,128)} %dg2_ref.1) | copy-start | bytes 786436
  7.5 2.4 %copy-start.3 = (bf16[256,256]{1,0:T(8,128)(2,1)S(1)}, bf16[256,256]{1,0:T(8,128)(2,1)}, u32[]{:S(2)}) copy-start(bf16[256,256]{1,0:T(8,128)(2,1)} %cl_ref.1) | copy-start | bytes 393220
  7.5 2.4 %copy-start.4 = (bf16[256,256]{1,0:T(8,128)(2,1)S(1)}, bf16[256,256]{1,0:T(8,128)(2,1)}, u32[]{:S(2)}) copy-start(bf16[256,256]{1,0:T(8,128)(2,1)} %cu_ref.1) | copy-start | bytes 393220

commit v2 on v1

--- a/solution.py
+++ b/solution.py
@@ -13,6 +13,7 @@
 TWO = 4
 XH = 2
 CORES = 2
+XL = 2
 MESH = pl.DeviceIdType.MESH
 F32 = jnp.float32
 BF16 = jnp.bfloat16
@@ -71,14 +72,24 @@
     Dall,
     tail,
     sem_sel,
-    gz_s,
-    gz_r,
-    gx_s,
-    gx_r,
-    gc_s,
-    gc_r,
-    xg_s,
-    xg_r,
+    xs_s,
+    xs_r,
+    xy_s,
+    xy_r,
+    ap_s,
+    am_s,
+    a_r,
+    bp_s,
+    bm_s,
+    b_r,
+    ax_s,
+    ax_r,
+    ac_s,
+    ac_r,
+    bc_s,
+    bc_r,
+    bx_s,
+    bx_r,
     cs_s,
     cs_r,
     rx_s,
@@ -109,6 +120,9 @@
     k = lax.rem(c, CORES)
     z = lax.rem(c // CORES, Z)
     xh = c // (CORES * Z)
+    Y = R // XL
+    y = r // XL
+    xl = lax.rem(r, XL)
 
     def col_of(xh_, z_, k_):
         return (xh_ * Z + z_) * CORES + k_
@@ -164,35 +178,100 @@
     loop(R - 1, greet_r)
 
     for half in range(2):
-        G[half, c] = own_u[half]
-        XG[half, r] = own_x[half]
+        G[half, xh, z, k] = own_u[half]
+        XG[half, y, xl] = own_x[half]
 
     pl.semaphore_wait(barrier, 2 + (Z - 1) + (R - 1))
 
-    def gz(src_z, to_z):
-        slot = col_of(xh, src_z, k)
-        return rcopy(G.at[:, slot], G.at[:, slot], gz_s.at[to_z], gz_r.at[src_z], z_dev(to_z))
-
-    def gx(src_xh, src_z):
-        slot = col_of(src_xh, src_z, k)
-        return rcopy(G.at[:, slot], G.at[:, slot], gx_s.at[src_z], gx_r.at[src_z], x_dev)
-
-    def gc(src_xh, src_z, src_k):
-        slot = col_of(src_xh, src_z, src_k)
-        sem = src_xh * Z + src_z
-        return rcopy(G.at[:, slot], G.at[:, slot], gc_s.at[sem], gc_r.at[sem], core_dev)
-
-    def xg(src_r, to_r):
+    near = (y * XL + 1 - xl, c)
+
+    def xgx(src_xl):
+        return rcopy(XG.at[:, y, src_xl], XG.at[:, y, src_xl], xs_s.at[0], xs_r.at[0], near)
+
+    def y_at(i):
+        return lax.rem(y + 1 + i, Y)
+
+    def xgy(src_y, to_y):
         return rcopy(
-            XG.at[:, src_r], XG.at[:, src_r], xg_s.at[to_r], xg_r.at[src_r], row_dev(to_r)
+            XG.at[:, src_y], XG.at[:, src_y], xy_s.at[to_y], xy_r.at[src_y], (to_y * XL + xl, c)
         )
 
-    loop(R - 1, lambda i: xg(r, r_at(i)).start())
-    loop(Z - 1, lambda i: gz(z, z_at(i)).start())
-    gx(xh, z).start()
-    gc(xh, z, k).start()
-
-    loop(R - 1, lambda i: xg(r_at(i), r).wait_recv())
+    far_p, far_m = Z // 2, Z // 2 - 1
+    z_next = lax.rem(z + 1, Z)
+    z_prev = lax.rem(z + Z - 1, Z)
+
+    def behind(t):
+        return lax.rem(z + Z - 1 - t, Z)
+
+    def ahead(t):
+        return lax.rem(z + 1 + t, Z)
+
+    def a_ring(src_z, sems, to):
+        block = G.at[0, xh, src_z, k]
+        return rcopy(block, block, sems.at[src_z], a_r.at[src_z], z_dev(to))
+
+    def b_ring(src_z, sems, to):
+        block = G.at[1, :, src_z, k]
+        return rcopy(block, block, sems.at[src_z], b_r.at[src_z], z_dev(to))
+
+    def a_x(src_xh, src_z):
+        block = G.at[0, src_xh, src_z, k]
+        return rcopy(block, block, ax_s.at[src_z], ax_r.at[src_z], x_dev)
+
+    def a_core(src_xh, src_z, src_k):
+        block = G.at[0, src_xh, src_z, src_k]
+        n = src_xh * Z + src_z
+        return rcopy(block, block, ac_s.at[n], ac_r.at[n], core_dev)
+
+    def b_core(src_z, src_k):
+        block = G.at[1, :, src_z, src_k]
+        return rcopy(block, block, bc_s.at[src_z], bc_r.at[src_z], core_dev)
+
+    def b_x(src_xh):
+        block = G.at[1, src_xh, z, k]
+        return rcopy(block, block, bx_s.at[0], bx_r.at[0], x_dev)
+
+    b_x(xh).start()
+    xgx(xl).start()
+    a_ring(z, ap_s, z_next).start()
+    if far_m > 0:
+        a_ring(z, am_s, z_prev).start()
+    a_x(xh, z).start()
+    a_core(xh, z, k).start()
+    xgx(1 - xl).wait_recv()
+    loop(Y - 1, lambda i: xgy(y, y_at(i)).start())
+    b_x(1 - xh).wait_recv()
+    b_ring(z, bp_s, z_next).start()
+    if far_m > 0:
+        b_ring(z, bm_s, z_prev).start()
+    b_core(z, k).start()
+    for t in range(far_p):
+        zz = behind(t)
+        a_ring(zz, ap_s, z_next).wait_recv()
+        if t < far_p - 1:
+            a_ring(zz, ap_s, z_next).start()
+        a_x(xh, zz).start()
+        a_core(xh, zz, k).start()
+        if t < far_m:
+            zz = ahead(t)
+            a_ring(zz, am_s, z_prev).wait_recv()
+            if t < far_m - 1:
+                a_ring(zz, am_s, z_prev).start()
+            a_x(xh, zz).start()
+            a_core(xh, zz, k).start()
+        zz = behind(t)
+        b_ring(zz, bp_s, z_next).wait_recv()
+        if t < far_p - 1:
+            b_ring(zz, bp_s, z_next).start()
+        b_core(zz, k).start()
+        if t < far_m:
+            zz = ahead(t)
+            b_ring(zz, bm_s, z_prev).wait_recv()
+            if t < far_m - 1:
+                b_ring(zz, bm_s, z_prev).start()
+            b_core(zz, k).start()
+
+    loop(Y - 1, lambda i: xgy(y_at(i), y).wait_recv())
     x1t = XG[0].reshape(W, ncol)
     lct = XG[1].reshape(W, ncol)
     clt = cl_ref[...].astype(F32).T.astype(BF16)
@@ -209,29 +288,22 @@
     sel2_copy.wait()
 
     def lower(m):
-        first = sel[pl.ds(pl.multiple_of(m * (2 * s1), 16), 2 * s1), :]
+        first = sel[pl.ds(pl.multiple_of(m * (2 * s1), 16), 4 * s1), :]
         p1 = mm(first, X[:, 0:W])
-        Pm[m, 0, 0:s1, :] = p1[0:s1]
-        Pm[m, 1, 0:s1, :] = p1[s1:]
-        rows = sel2[pl.ds(pl.multiple_of(m * (2 * s2), 16), 2 * s2), :]
+        rows = sel2[pl.ds(pl.multiple_of(m * (2 * s2), 16), 4 * s2), :]
         p2 = mm(rows, X[:, W : 2 * W]) + mm(rows, X[:, 2 * W : 3 * W])
-        Pm[m, 0, s1 : s1 + s2, :] = p2[0:s2]
-        Pm[m, 1, s1 : s1 + s2, :] = p2[s2:]
-        cs(m).start()
-
-    loop(Z, lambda i: lower((1 - xh) * Z + z_at(i)))
-
-    def pass_on(i):
-        lower(xh * Z + z_at(i))
-
-        @pl.when(i < Z - 1)
-        def _():
-            zz = z_at(i)
-            gz(zz, z).wait_recv()
-            gx(xh, zz).start()
-            gc(xh, zz, k).start()
-
-    loop(Z, pass_on)
+        for j in range(2):
+            for core in range(CORES):
+                n = 2 * j + core
+                Pm[m + j, core, 0:s1, :] = p1[n * s1 : (n + 1) * s1]
+                Pm[m + j, core, s1 : s1 + s2, :] = p2[n * s2 : (n + 1) * s2]
+            cs(m + j).start()
+
+    def pair_at(i):
+        return 2 * lax.rem(z // 2 + 1 + i, Z // 2)
+
+    loop(Z // 2, lambda i: lower((1 - xh) * Z + pair_at(i)))
+    loop(Z // 2, lambda i: lower(xh * Z + pair_at(i)))
 
     def rx(zz):
         return rcopy(xs.at[zz], xr.at[zz], rx_s.at[zz], rx_r.at[zz], x_dev)
@@ -248,6 +320,42 @@
 
     loop(Z, to_x)
 
+    def over(i):
+        zz = z_at(i)
+        a_x(1 - xh, zz).wait_recv()
+        a_core(1 - xh, zz, k).start()
+
+    loop(Z, over)
+    loop(Z, lambda i: b_core(i, 1 - k).wait_recv())
+    loop(M, lambda i: a_core(i // Z, lax.rem(i, Z), 1 - k).wait_recv())
+    cu = cu_ref[...]
+    wide = 2 * B if nb1 % 2 == 0 else B
+
+    def second(j):
+        at = pl.ds(pl.multiple_of(j * wide, wide), wide)
+        up = G[0, :, :, :, :, at].reshape(W, wide)
+        uc = G[1, :, :, :, :, at].reshape(W, wide)
+        v = uc.astype(F32) - mm(cu, up)
+        hi = v.astype(BF16)
+        V[0, :, at] = up
+        V[1, :, at] = hi
+        V[2, :, at] = (v - hi.astype(F32)).astype(BF16)
+
+    loop(nb1 * B // wide, second)
+
+    def upper(j):
+        PU[j] = mm(V[j], sel[...])
+
+    loop(3, upper)
+    PU[1] = PU[1] + PU[2]
+    PUb[0] = PU[0].astype(BF16).reshape(R, uw, ncol)
+    PUb[1] = PU[1].astype(BF16).reshape(R, uw, ncol)
+
+    def pu(src_r, to_r):
+        return rcopy(PUb.at[:, to_r], ur_buf.at[:, src_r], pu_s.at[to_r], pu_r.at[src_r], row_dev(to_r))
+
+    loop(R - 1, lambda i: pu(r, r_at(i)).start())
+
     def to_z(i):
         zz = z_at(i)
         m = xh * Z + zz
@@ -264,56 +372,12 @@
         def _():
             own[...] = total
 
-        zg = lax.rem(z + i, Z)
-        gx(1 - xh, zg).wait_recv()
-        gc(1 - xh, zg, k).start()
-
     loop(Z, to_z)
 
-    def all_in(i):
-        gc(i // Z, lax.rem(i, Z), 1 - k).wait_recv()
-
-    loop(M, all_in)
-    cu = cu_ref[...]
-    wide = 2 * B if nb1 % 2 == 0 else B
-
-    def second(j):
-        at = pl.ds(pl.multiple_of(j * wide, wide), wide)
-        up = G[0, :, :, at].reshape(W, wide)
-        uc = G[1, :, :, at].reshape(W, wide)
-        v = uc.astype(F32) - mm(cu, up)
-        hi = v.astype(BF16)
-        V[0, :, at] = up
-        V[1, :, at] = hi
-        V[2, :, at] = (v - hi.astype(F32)).astype(BF16)
-
-    loop(nb1 * B // wide, second)
-
-    def upper(j):
-        PU[j] = mm(V[j], sel[...])
-
-    loop(3, upper)
-    PU[1] = PU[1] + PU[2]
-    PUb[0] = PU[0].astype(BF16).reshape(R, uw, ncol)
-    PUb[1] = PU[1].astype(BF16).reshape(R, uw, ncol)
-
-    def pu(src_r, to_r):
-        return rcopy(PUb.at[:, to_r], ur_buf.at[:, src_r], pu_s.at[to_r], pu_r.at[src_r], row_dev(to_r))
-
-    loop(R - 1, lambda i: pu(r, r_at(i)).start())
 
     tail[...] = dg2_ref[...] + exact(
         cu.astype(F32), exact(dg1_ref[...], cl_ref[...].astype(F32))
     )
-
-    def from_z(i):
-        zz = z_at(i)
-        rz(zz, z).wait_recv()
-        own[...] = own[...] + zr[zz].astype(F32)
-
-    loop(Z - 1, from_z)
-    l1_out[...] = (-own[0:s1, :]).astype(BF16)
-    l2_out[...] = (-own[s1 : s1 + s2, :]).astype(BF16)
 
     mine = pl.ds(pl.multiple_of(r * uw, 16), uw)
 
@@ -338,16 +402,16 @@
     d_x = rcopy(dxs, drx, d_s.at[1], d_r.at[1], x_dev)
     d_x.start()
     d_x.wait_recv()
-    dz[z] = dxs[...] + drx[...]
+    dz[z] = (dxs[...] + drx[...]).astype(BF16)
 
     def dzc(src_z, to_z):
         return rcopy(dz.at[src_z], dz.at[src_z], dz_s.at[to_z], dz_r.at[src_z], z_dev(to_z))
 
     loop(Z - 1, lambda i: dzc(z, z_at(i)).start())
     loop(Z - 1, lambda i: dzc(z_at(i), z).wait_recv())
-    total = dz[0]
+    total = dz[0].astype(F32)
     for i in range(1, Z):
-        total = total + dz[i]
+        total = total + dz[i].astype(F32)
     Dall[k, r] = total
 
     def drow(src_r, to_r):
@@ -356,6 +420,15 @@
         )
 
     loop(R - 1, lambda i: drow(r, r_at(i)).start())
+    def from_z(i):
+        zz = z_at(i)
+        rz(zz, z).wait_recv()
+        own[...] = own[...] + zr[zz].astype(F32)
+
+    loop(Z - 1, from_z)
+    l1_out[...] = (-own[0:s1, :]).astype(BF16)
+    l2_out[...] = (-own[s1 : s1 + s2, :]).astype(BF16)
+
     loop(R - 1, lambda i: drow(r_at(i), r).wait_recv())
 
     def d_both(src_k):
@@ -368,24 +441,32 @@
 
     def left_z(i):
         zz = z_at(i)
-        gz(z, zz).wait_send()
         rz(z, zz).wait_send()
         dzc(z, zz).wait_send()
 
     def left_r(i):
         rr = r_at(i)
-        xg(r, rr).wait_send()
         pu(r, rr).wait_send()
         drow(r, rr).wait_send()
 
     def left_x(i):
-        gx(xh, i).wait_send()
+        a_x(xh, i).wait_send()
         rx(i).wait_send()
+        b_core(i, k).wait_send()
 
     def left_c(i):
-        gc(i // Z, lax.rem(i, Z), k).wait_send()
+        a_core(i // Z, lax.rem(i, Z), k).wait_send()
         cs(i).wait_send()
 
+    b_x(xh).wait_send()
+    xgx(xl).wait_send()
+    loop(Y - 1, lambda i: xgy(y, y_at(i)).wait_send())
+    for t in range(far_p):
+        a_ring(lax.rem(z + Z - t, Z), ap_s, z_next).wait_send()
+        b_ring(lax.rem(z + Z - t, Z), bp_s, z_next).wait_send()
+    for t in range(far_m):
+        a_ring(lax.rem(z + t, Z), am_s, z_prev).wait_send()
+        b_ring(lax.rem(z + t, Z), bm_s, z_prev).wait_send()
     loop(Z - 1, left_z)
     loop(R - 1, left_r)
     loop(Z, left_x)
@@ -526,9 +607,9 @@
         scratch_shapes=[
             pltpu.VMEM((nb1 * B, ncol), BF16),
             pltpu.VMEM((runs * TWO * B, ncol), BF16),
-            pltpu.VMEM((2, C, ur, nb1 * B), BF16),
+            pltpu.VMEM((2, XH, Z, CORES, ur, nb1 * B), BF16),
             pltpu.VMEM((3, W, nb1 * B), BF16),
-            pltpu.VMEM((2, R, lw, ncol), BF16),
+            pltpu.VMEM((2, R // XL, XL, lw, ncol), BF16),
             pltpu.VMEM((ncol, 3 * W), BF16),
             pltpu.VMEM((M, 2, sh, W), F32),
             pltpu.VMEM((M, sh, W), F32),
@@ -544,11 +625,13 @@
             pltpu.VMEM((uw, W), F32),
             pltpu.VMEM((uw, W), F32),
             pltpu.VMEM((uw, W), F32),
-            pltpu.VMEM((Z, uw, W), F32),
+            pltpu.VMEM((Z, uw, W), BF16),
             pltpu.VMEM((2, R, uw, W), F32),
             pltpu.VMEM((W, W), F32),
         ]
-        + [dma((n,)) for n in (2, Z, Z, Z, Z, M, M, R, R, M, M, Z, Z, Z, Z, R, R, 3, 3, Z, Z, R, R)],
+        + [dma((n,)) for n in (2, 1, 1, R // XL, R // XL)]
+        + [dma((n,)) for n in (Z, Z, Z, Z, Z, Z, Z, Z, M, M, Z, Z, 1, 1)]
+        + [dma((n,)) for n in (M, M, Z, Z, Z, Z, R, R, 3, 3, Z, Z, R, R)],
         compiler_params=pltpu.CompilerParams(
             collective_id=0, has_side_effects=True, vmem_limit_bytes=40 * 2**20
         ),

time: 105 us -> 92 us (0.88)
  Pallas kernels: 93 us -> 80.2 us
    pallas_call x1, Pallas kernels: 90.7 us -> 77.9 us  [on_device(): pl.pallas_call(functools.partial(kernel, R, C, W), out_shape=(jax.ShapeDt...]
where the time goes in v2:
time: 92 us; the launch traced here: 91.6 us
  Pallas kernels  80.2 us (87%)
  local copies, waits for them, and re-layouts  10.7 us (12%)
    pallas_call x1, Pallas kernels, on_device(): pl.pallas_call(functools.partial(kernel, R, C, W), out_shape=(jax.ShapeDt...  77.9 us
    unnamed x28, local copies, waits for them, and re-layouts  10.7 us
    pallas_call x1, Pallas kernels, on_device(): pl.pallas_call(functools.partial(pick, R, C), out_shape=(jax.ShapeDtypeSt...  2.32 us

profile of v2, /device:TPU:1, one launch (start us, length us, event | category | flops | bytes accessed | tf_op | source)
XLA Modules:
  0.0 91.6 jit_solution(516587800196046240)
XLA Ops:
  0.6 0.0 copy-start
  0.6 2.3 %copy-done = bf16[3072,768]{1,0:T(8,128)(2,1)S(1)} copy-done((bf16[3072,768]{1,0:T(8,128)(2,1)S(1)}, bf16[3072,768]{1,0:T(8,128)(2,1)}, u32[]{:S(2)}) %copy-start) | copy-done | bytes 4718616
  3.0 0.0 copy-start.5
  3.0 0.8 copy-done.5
  3.8 0.0 copy-start.6
  3.8 0.8 copy-done.6
  4.6 0.0 copy-start.7
  4.6 0.8 copy-done.7
  5.4 0.0 copy-start.8
  5.4 0.8 copy-done.8
  6.2 0.7 copy-done.9
  6.9 0.7 copy-done.10
  7.5 2.3 %pick.1 = (bf16[2560,640]{1,0:T(8,128)(2,1)S(1)}, bf16[2048,640]{1,0:T(8,128)(2,1)S(1)}, bf16[2,8,2560]{2,1,0:T(8,128)(2,1)S(1)}, bf16[2,32,640]{2,1,0:T(8,128)(2,1)S(1)}, bf16[640,512]{1,0:T(8,128)(2,1)S(1)}) custom-call(s32[160]{0:T(256)S(1)} %copy-done.9, s32[128]{0:T(128)S(1)} %copy-done.10, bf16[3072,768]{1,0:T(8,128)(2,1)S(1)} %copy-done, ...), custom_call_target="tpu_custom_call" | custom-call | tf_op jit(solution)/shard_map/pick/pallas_call | solution.py:581
  9.8 0.0 copy-done.1
  9.9 0.0 copy-done.2
  9.9 0.0 copy-done.3
  9.9 0.0 copy-done.4
  9.9 77.9 %panels.1 = (bf16[80,256]{1,0:T(8,128)(2,1)S(1)}, bf16[32,640]{1,0:T(8,128)(2,1)S(1)}, f32[256,256]{1,0:T(8,128)S(1)}, bf16[64,256]{1,0:T(8,128)(2,1)S(1)}, bf16...) custom-call(bf16[2560,640]{1,0:T(8,128)(2,1)S(1)} %get-tuple-element.11.sel_any, ...), custom_call_target="tpu_custom_call" | custom-call | tf_op jit(solution)/shard_map/panels/pallas_call | solution.py:595
  87.8 0.6 copy.23
  88.4 0.6 copy.24
  89.0 0.7 copy.25
  89.7 0.6 copy.26
  90.3 0.6 copy.27
  90.9 0.7 copy.28
  (6 shorter events, 0.0 us)
Async XLA Ops:
  0.6 2.3 %copy-start = (bf16[3072,768]{1,0:T(8,128)(2,1)S(1)}, bf16[3072,768]{1,0:T(8,128)(2,1)}, u32[]{:S(2)}) copy-start(bf16[3072,768]{1,0:T(8,128)(2,1)} %sep.1) | copy-start | bytes 14155780
  3.0 0.8 copy-start.5
  3.8 0.8 copy-start.6
  4.6 0.8 copy-start.7
  5.4 0.8 copy-start.8
  6.2 0.7 copy-start.9
  6.8 0.7 copy-start.10
  7.5 2.3 %copy-start.1 = (f32[256,256]{1,0:T(8,128)S(1)}, f32[256,256]{1,0:T(8,128)}, u32[]{:S(2)}) copy-start(f32[256,256]{1,0:T(8,128)} %dg1_ref.1) | copy-start | bytes 786436
  7.5 2.4 %copy-start.2 = (f32[256,256]{1,0:T(8,128)S(1)}, f32[256,256]{1,0:T(8,128)}, u32[]{:S(2)}) copy-start(f32[256,256]{1,0:T(8,128)} %dg2_ref.1) | copy-start | bytes 786436
  7.5 2.4 %copy-start.3 = (bf16[256,256]{1,0:T(8,128)(2,1)S(1)}, bf16[256,256]{1,0:T(8,128)(2,1)}, u32[]{:S(2)}) copy-start(bf16[256,256]{1,0:T(8,128)(2,1)} %cl_ref.1) | copy-start | bytes 393220
  7.5 2.4 %copy-start.4 = (bf16[256,256]{1,0:T(8,128)(2,1)S(1)}, bf16[256,256]{1,0:T(8,128)(2,1)}, u32[]{:S(2)}) copy-start(bf16[256,256]{1,0:T(8,128)(2,1)} %cu_ref.1) | copy-start | bytes 393220

commit v3 on v2

--- a/solution.py
+++ b/solution.py
@@ -66,8 +66,6 @@
     ur_buf,
     dd,
     drc,
-    dxs,
-    drx,
     dz,
     Dall,
     tail,
@@ -104,6 +102,8 @@
     dz_r,
     dr_s,
     dr_r,
+    df_s,
+    df_r,
 ):
     Z = C // (XH * CORES)
     runs = C // R
@@ -129,6 +129,7 @@
 
     core_dev = (r, col_of(xh, z, 1 - k))
     x_dev = (r, col_of(1 - xh, z, k))
+    cross_dev = (r, col_of(1 - xh, z, 1 - k))
 
     def z_at(i):
         return lax.rem(z + 1 + i, Z)
@@ -167,6 +168,7 @@
     barrier = pltpu.get_barrier_semaphore()
     pl.semaphore_signal(barrier, inc=1, device_id=core_dev, device_id_type=MESH)
     pl.semaphore_signal(barrier, inc=1, device_id=x_dev, device_id_type=MESH)
+    pl.semaphore_signal(barrier, inc=1, device_id=cross_dev, device_id_type=MESH)
 
     def greet_z(i):
         pl.semaphore_signal(barrier, inc=1, device_id=z_dev(z_at(i)), device_id_type=MESH)
@@ -181,7 +183,7 @@
         G[half, xh, z, k] = own_u[half]
         XG[half, y, xl] = own_x[half]
 
-    pl.semaphore_wait(barrier, 2 + (Z - 1) + (R - 1))
+    pl.semaphore_wait(barrier, 3 + (Z - 1) + (R - 1))
 
     near = (y * XL + 1 - xl, c)
 
@@ -245,7 +247,7 @@
     if far_m > 0:
         b_ring(z, bm_s, z_prev).start()
     b_core(z, k).start()
-    for t in range(far_p):
+    def a_step(t):
         zz = behind(t)
         a_ring(zz, ap_s, z_next).wait_recv()
         if t < far_p - 1:
@@ -259,6 +261,8 @@
                 a_ring(zz, am_s, z_prev).start()
             a_x(xh, zz).start()
             a_core(xh, zz, k).start()
+
+    def b_step(t):
         zz = behind(t)
         b_ring(zz, bp_s, z_next).wait_recv()
         if t < far_p - 1:
@@ -271,16 +275,6 @@
                 b_ring(zz, bm_s, z_prev).start()
             b_core(zz, k).start()
 
-    loop(Y - 1, lambda i: xgy(y_at(i), y).wait_recv())
-    x1t = XG[0].reshape(W, ncol)
-    lct = XG[1].reshape(W, ncol)
-    clt = cl_ref[...].astype(F32).T.astype(BF16)
-    x2 = (lct.astype(F32) - mm(clt, x1t)).T
-    x2hi = x2.astype(BF16)
-    X[:, 0:W] = x1t.astype(F32).T.astype(BF16)
-    X[:, W : 2 * W] = x2hi
-    X[:, 2 * W : 3 * W] = (x2 - x2hi.astype(F32)).astype(BF16)
-
     def cs(m):
         return rcopy(Pm.at[m, 1 - k], cr.at[m], cs_s.at[m], cs_r.at[m], core_dev)
 
@@ -302,8 +296,42 @@
     def pair_at(i):
         return 2 * lax.rem(z // 2 + 1 + i, Z // 2)
 
-    loop(Z // 2, lambda i: lower((1 - xh) * Z + pair_at(i)))
-    loop(Z // 2, lambda i: lower(xh * Z + pair_at(i)))
+    def lower_at(n):
+        lower(jnp.where(n < Z // 2, 1 - xh, xh) * Z + pair_at(lax.rem(n, Z // 2)))
+
+    a_step(0)
+    if far_p > 1:
+        a_step(1)
+    b_step(0)
+    loop(Y - 1, lambda i: xgy(y_at(i), y).wait_recv())
+    x1t = XG[0].reshape(W, ncol)
+    lct = XG[1].reshape(W, ncol)
+    clt = cl_ref[...].astype(F32).T.astype(BF16)
+    x2 = (lct.astype(F32) - mm(clt, x1t)).T
+    x2hi = x2.astype(BF16)
+    X[:, 0:W] = x1t.astype(F32).T.astype(BF16)
+    X[:, W : 2 * W] = x2hi
+    X[:, 2 * W : 3 * W] = (x2 - x2hi.astype(F32)).astype(BF16)
+
+    first = 0
+    for t in range(1, far_p):
+        if t + 1 < far_p:
+            a_step(t + 1)
+        share = Z // (2 * far_p)
+        loop(share, lambda i, first=first: lower_at(first + i))
+        first += share
+        if t < far_p - 1:
+            b_step(t)
+            loop(share, lambda i, first=first: lower_at(first + i))
+            first += share
+
+    def over(i):
+        zz = z_at(i)
+        a_x(1 - xh, zz).wait_recv()
+        a_core(1 - xh, zz, k).start()
+
+    loop(Z, over)
+    loop(Z - first, lambda i: lower_at(first + i))
 
     def rx(zz):
         return rcopy(xs.at[zz], xr.at[zz], rx_s.at[zz], rx_r.at[zz], x_dev)
@@ -320,14 +348,23 @@
 
     loop(Z, to_x)
 
-    def over(i):
-        zz = z_at(i)
-        a_x(1 - xh, zz).wait_recv()
-        a_core(1 - xh, zz, k).start()
-
-    loop(Z, over)
+    def pu(j, src_r, to_r):
+        return rcopy(
+            PUb.at[j, to_r],
+            ur_buf.at[j, src_r],
+            pu_s.at[j, to_r],
+            pu_r.at[j, src_r],
+            row_dev(to_r),
+        )
+
+    loop(M, lambda i: a_core(i // Z, lax.rem(i, Z), 1 - k).wait_recv())
+    PU[0] = mm(G[0].reshape(W, nb1 * B), sel[...])
+    PUb[0] = PU[0].astype(BF16).reshape(R, uw, ncol)
+    loop(R - 1, lambda i: pu(0, r, r_at(i)).start())
+
+    if far_p > 1:
+        b_step(far_p - 1)
     loop(Z, lambda i: b_core(i, 1 - k).wait_recv())
-    loop(M, lambda i: a_core(i // Z, lax.rem(i, Z), 1 - k).wait_recv())
     cu = cu_ref[...]
     wide = 2 * B if nb1 % 2 == 0 else B
 
@@ -337,24 +374,18 @@
         uc = G[1, :, :, :, :, at].reshape(W, wide)
         v = uc.astype(F32) - mm(cu, up)
         hi = v.astype(BF16)
-        V[0, :, at] = up
-        V[1, :, at] = hi
-        V[2, :, at] = (v - hi.astype(F32)).astype(BF16)
+        V[0, :, at] = hi
+        V[1, :, at] = (v - hi.astype(F32)).astype(BF16)
 
     loop(nb1 * B // wide, second)
 
-    def upper(j):
-        PU[j] = mm(V[j], sel[...])
-
-    loop(3, upper)
+    def both(j):
+        PU[1 + j] = mm(V[j], sel[...])
+
+    loop(2, both)
     PU[1] = PU[1] + PU[2]
-    PUb[0] = PU[0].astype(BF16).reshape(R, uw, ncol)
     PUb[1] = PU[1].astype(BF16).reshape(R, uw, ncol)
-
-    def pu(src_r, to_r):
-        return rcopy(PUb.at[:, to_r], ur_buf.at[:, src_r], pu_s.at[to_r], pu_r.at[src_r], row_dev(to_r))
-
-    loop(R - 1, lambda i: pu(r, r_at(i)).start())
+    loop(R - 1, lambda i: pu(1, r, r_at(i)).start())
 
     def to_z(i):
         zz = z_at(i)
@@ -383,26 +414,35 @@
 
     def from_r(i):
         rr = r_at(i)
-        pu(rr, r).wait_recv()
-        PU[0, mine, :] = PU[0, mine, :] + ur_buf[0, rr].astype(F32)
-        PU[1, mine, :] = PU[1, mine, :] + ur_buf[1, rr].astype(F32)
+        for j in range(2):
+            pu(j, rr, r).wait_recv()
+            PU[j, mine, :] = PU[j, mine, :] + ur_buf[j, rr].astype(F32)
 
     loop(R - 1, from_r)
     u1 = (-PU[0, mine, :]).astype(BF16)
     u2 = (-PU[1, mine, :]).astype(BF16)
     dd[0] = mm(u1, X[:, 0:W])
     dd[1] = mm(u2, X[:, W : 2 * W]) + mm(u2, X[:, 2 * W : 3 * W])
-    d_core = rcopy(dd.at[1 - k], drc, d_s.at[0], d_r.at[0], core_dev)
-    d_core.start()
+    me = xh * CORES + k
+
+    def d_four(src, half, to_, dev):
+        return rcopy(dd.at[half], drc.at[src], d_s.at[to_], d_r.at[src], dev)
+
+    core_at, x_at, cross_at = xh * CORES + 1 - k, (1 - xh) * CORES + k, (1 - xh) * CORES + 1 - k
+    sends = (
+        d_four(me, 1 - k, core_at, core_dev),
+        d_four(me, k, x_at, x_dev),
+        d_four(me, 1 - k, cross_at, cross_dev),
+    )
+    for send in sends:
+        send.start()
+    drc[me] = dd[k]
     u1_out[...] = u1
     u2_out[...] = mm(u2, pick_cols[...]).astype(BF16)
 
-    d_core.wait_recv()
-    dxs[...] = dd[k] + drc[...]
-    d_x = rcopy(dxs, drx, d_s.at[1], d_r.at[1], x_dev)
-    d_x.start()
-    d_x.wait_recv()
-    dz[z] = (dxs[...] + drx[...]).astype(BF16)
+    for src in (core_at, x_at, cross_at):
+        d_four(src, k, me, x_dev).wait_recv()
+    dz[z] = ((drc[0] + drc[1]) + (drc[2] + drc[3])).astype(BF16)
 
     def dzc(src_z, to_z):
         return rcopy(dz.at[src_z], dz.at[src_z], dz_s.at[to_z], dz_r.at[src_z], z_dev(to_z))
@@ -419,7 +459,12 @@
             Dall.at[k, src_r], Dall.at[k, src_r], dr_s.at[to_r], dr_r.at[src_r], row_dev(to_r)
         )
 
+    def d_core(src_r, src_k):
+        block = Dall.at[src_k, src_r]
+        return rcopy(block, block, df_s.at[src_r], df_r.at[src_r], core_dev)
+
     loop(R - 1, lambda i: drow(r, r_at(i)).start())
+    d_core(r, k).start()
     def from_z(i):
         zz = z_at(i)
         rz(zz, z).wait_recv()
@@ -429,13 +474,14 @@
     l1_out[...] = (-own[0:s1, :]).astype(BF16)
     l2_out[...] = (-own[s1 : s1 + s2, :]).astype(BF16)
 
-    loop(R - 1, lambda i: drow(r_at(i), r).wait_recv())
-
-    def d_both(src_k):
-        return rcopy(Dall.at[src_k], Dall.at[src_k], d_s.at[2], d_r.at[2], core_dev)
-
-    d_both(k).start()
-    d_both(1 - k).wait_recv()
+
+    def from_row(i):
+        rr = r_at(i)
+        drow(rr, r).wait_recv()
+        d_core(rr, k).start()
+
+    loop(R - 1, from_row)
+    loop(R, lambda i: d_core(i, 1 - k).wait_recv())
     d1_out[...] = dg1_ref[...] - Dall[0].reshape(W, W)
     d2_out[...] = tail[...] - Dall[1].reshape(W, W)
 
@@ -446,7 +492,8 @@
 
     def left_r(i):
         rr = r_at(i)
-        pu(r, rr).wait_send()
+        pu(0, r, rr).wait_send()
+        pu(1, r, rr).wait_send()
         drow(r, rr).wait_send()
 
     def left_x(i):
@@ -471,9 +518,9 @@
     loop(R - 1, left_r)
     loop(Z, left_x)
     loop(M, left_c)
-    d_core.wait_send()
-    d_x.wait_send()
-    d_both(k).wait_send()
+    loop(R, lambda i: d_core(i, k).wait_send())
+    for send in sends:
+        send.wait_send()
 
 
 def pick(
@@ -608,7 +655,7 @@
             pltpu.VMEM((nb1 * B, ncol), BF16),
             pltpu.VMEM((runs * TWO * B, ncol), BF16),
             pltpu.VMEM((2, XH, Z, CORES, ur, nb1 * B), BF16),
-            pltpu.VMEM((3, W, nb1 * B), BF16),
+            pltpu.VMEM((2, W, nb1 * B), BF16),
             pltpu.VMEM((2, R // XL, XL, lw, ncol), BF16),
             pltpu.VMEM((ncol, 3 * W), BF16),
             pltpu.VMEM((M, 2, sh, W), F32),
@@ -622,16 +669,16 @@
             pltpu.VMEM((2, R, uw, ncol), BF16),
             pltpu.VMEM((2, R, uw, ncol), BF16),
             pltpu.VMEM((2, uw, W), F32),
-            pltpu.VMEM((uw, W), F32),
-            pltpu.VMEM((uw, W), F32),
-            pltpu.VMEM((uw, W), F32),
+            pltpu.VMEM((XH * CORES, uw, W), F32),
             pltpu.VMEM((Z, uw, W), BF16),
             pltpu.VMEM((2, R, uw, W), F32),
             pltpu.VMEM((W, W), F32),
         ]
         + [dma((n,)) for n in (2, 1, 1, R // XL, R // XL)]
         + [dma((n,)) for n in (Z, Z, Z, Z, Z, Z, Z, Z, M, M, Z, Z, 1, 1)]
-        + [dma((n,)) for n in (M, M, Z, Z, Z, Z, R, R, 3, 3, Z, Z, R, R)],
+        + [dma((n,)) for n in (M, M, Z, Z, Z, Z)]
+        + [dma((2, R)), dma((2, R))]
+        + [dma((n,)) for n in (4, 4, Z, Z, R, R, R, R)],
         compiler_params=pltpu.CompilerParams(
             collective_id=0, has_side_effects=True, vmem_limit_bytes=40 * 2**20
         ),

time: 92 us -> 88.7 us (0.964)
  Pallas kernels: 80.2 us -> 76.9 us
    pallas_call x1, Pallas kernels: 77.9 us -> 74.6 us  [on_device(): pl.pallas_call(functools.partial(kernel, R, C, W), out_shape=(jax.ShapeDt...]
where the time goes in v3:
time: 88.7 us; the launch traced here: 88.3 us
  Pallas kernels  76.9 us (87%)
  local copies, waits for them, and re-layouts  10.7 us (12%)
    pallas_call x1, Pallas kernels, on_device(): pl.pallas_call(functools.partial(kernel, R, C, W), out_shape=(jax.ShapeDt...  74.6 us
    unnamed x28, local copies, waits for them, and re-layouts  10.7 us
    pallas_call x1, Pallas kernels, on_device(): pl.pallas_call(functools.partial(pick, R, C), out_shape=(jax.ShapeDtypeSt...  2.32 us

profile of v3, /device:TPU:1, one launch (start us, length us, event | category | flops | bytes accessed | tf_op | source)
XLA Modules:
  0.0 88.3 jit_solution(4177982384300394019)
XLA Ops:
  0.6 0.0 copy-start
  0.6 2.3 %copy-done = bf16[3072,768]{1,0:T(8,128)(2,1)S(1)} copy-done((bf16[3072,768]{1,0:T(8,128)(2,1)S(1)}, bf16[3072,768]{1,0:T(8,128)(2,1)}, u32[]{:S(2)}) %copy-start) | copy-done | bytes 4718616
  3.0 0.0 copy-start.5
  3.0 0.8 copy-done.5
  3.8 0.0 copy-start.6
  3.8 0.8 copy-done.6
  4.6 0.0 copy-start.7
  4.6 0.8 copy-done.7
  5.4 0.0 copy-start.8
  5.4 0.8 copy-done.8
  6.2 0.7 copy-done.9
  6.9 0.7 copy-done.10
  7.5 2.3 %pick.1 = (bf16[2560,640]{1,0:T(8,128)(2,1)S(1)}, bf16[2048,640]{1,0:T(8,128)(2,1)S(1)}, bf16[2,8,2560]{2,1,0:T(8,128)(2,1)S(1)}, bf16[2,32,640]{2,1,0:T(8,128)(2,1)S(1)}, bf16[640,512]{1,0:T(8,128)(2,1)S(1)}) custom-call(s32[160]{0:T(256)S(1)} %copy-done.9, s32[128]{0:T(128)S(1)} %copy-done.10, bf16[3072,768]{1,0:T(8,128)(2,1)S(1)} %copy-done, ...), custom_call_target="tpu_custom_call" | custom-call | tf_op jit(solution)/shard_map/pick/pallas_call | solution.py:628
  9.8 0.0 copy-done.1
  9.9 0.0 copy-done.2
  9.9 0.0 copy-done.3
  9.9 0.0 copy-done.4
  9.9 74.6 %panels.1 = (bf16[80,256]{1,0:T(8,128)(2,1)S(1)}, bf16[32,640]{1,0:T(8,128)(2,1)S(1)}, f32[256,256]{1,0:T(8,128)S(1)}, bf16[64,256]{1,0:T(8,128)(2,1)S(1)}, bf16...) custom-call(bf16[2560,640]{1,0:T(8,128)(2,1)S(1)} %get-tuple-element.11.sel_any, ...), custom_call_target="tpu_custom_call" | custom-call | tf_op jit(solution)/shard_map/panels/pallas_call | solution.py:642
  84.5 0.6 copy.23
  85.1 0.6 copy.24
  85.7 0.7 copy.25
  86.4 0.6 copy.26
  87.0 0.6 copy.27
  87.6 0.7 copy.28
  (6 shorter events, 0.0 us)
Async XLA Ops:
  0.6 2.3 %copy-start = (bf16[3072,768]{1,0:T(8,128)(2,1)S(1)}, bf16[3072,768]{1,0:T(8,128)(2,1)}, u32[]{:S(2)}) copy-start(bf16[3072,768]{1,0:T(8,128)(2,1)} %sep.1) | copy-start | bytes 14155780
  3.0 0.8 copy-start.5
  3.8 0.8 copy-start.6
  4.6 0.8 copy-start.7
  5.4 0.8 copy-start.8
  6.2 0.7 copy-start.9
  6.8 0.7 copy-start.10
  7.5 2.3 %copy-start.1 = (f32[256,256]{1,0:T(8,128)S(1)}, f32[256,256]{1,0:T(8,128)}, u32[]{:S(2)}) copy-start(f32[256,256]{1,0:T(8,128)} %dg1_ref.1) | copy-start | bytes 786436
  7.5 2.4 %copy-start.2 = (f32[256,256]{1,0:T(8,128)S(1)}, f32[256,256]{1,0:T(8,128)}, u32[]{:S(2)}) copy-start(f32[256,256]{1,0:T(8,128)} %dg2_ref.1) | copy-start | bytes 786436
  7.5 2.4 %copy-start.3 = (bf16[256,256]{1,0:T(8,128)(2,1)S(1)}, bf16[256,256]{1,0:T(8,128)(2,1)}, u32[]{:S(2)}) copy-start(bf16[256,256]{1,0:T(8,128)(2,1)} %cl_ref.1) | copy-start | bytes 393220
  7.5 2.4 %copy-start.4 = (bf16[256,256]{1,0:T(8,128)(2,1)S(1)}, bf16[256,256]{1,0:T(8,128)(2,1)}, u32[]{:S(2)}) copy-start(bf16[256,256]{1,0:T(8,128)(2,1)} %cu_ref.1) | copy-start | bytes 393220

commit v4 on v3

--- a/solution.py
+++ b/solution.py
@@ -300,9 +300,9 @@
         lower(jnp.where(n < Z // 2, 1 - xh, xh) * Z + pair_at(lax.rem(n, Z // 2)))
 
     a_step(0)
-    if far_p > 1:
-        a_step(1)
-    b_step(0)
+    for t in range(1, far_p):
+        a_step(t)
+        b_step(t - 1)
     loop(Y - 1, lambda i: xgy(y_at(i), y).wait_recv())
     x1t = XG[0].reshape(W, ncol)
     lct = XG[1].reshape(W, ncol)
@@ -313,17 +313,7 @@
     X[:, W : 2 * W] = x2hi
     X[:, 2 * W : 3 * W] = (x2 - x2hi.astype(F32)).astype(BF16)
 
-    first = 0
-    for t in range(1, far_p):
-        if t + 1 < far_p:
-            a_step(t + 1)
-        share = Z // (2 * far_p)
-        loop(share, lambda i, first=first: lower_at(first + i))
-        first += share
-        if t < far_p - 1:
-            b_step(t)
-            loop(share, lambda i, first=first: lower_at(first + i))
-            first += share
+    loop(Z // 2, lower_at)
 
     def over(i):
         zz = z_at(i)
@@ -331,7 +321,7 @@
         a_core(1 - xh, zz, k).start()
 
     loop(Z, over)
-    loop(Z - first, lambda i: lower_at(first + i))
+    loop(Z // 2, lambda i: lower_at(Z // 2 + i))
 
     def rx(zz):
         return rcopy(xs.at[zz], xr.at[zz], rx_s.at[zz], rx_r.at[zz], x_dev)
@@ -362,8 +352,7 @@
     PUb[0] = PU[0].astype(BF16).reshape(R, uw, ncol)
     loop(R - 1, lambda i: pu(0, r, r_at(i)).start())
 
-    if far_p > 1:
-        b_step(far_p - 1)
+    b_step(far_p - 1)
     loop(Z, lambda i: b_core(i, 1 - k).wait_recv())
     cu = cu_ref[...]
     wide = 2 * B if nb1 % 2 == 0 else B
@@ -596,6 +585,15 @@
         for t in range(TWO):
             hit = jnp.full((B, B), (two_at(c, t) == b).astype(jnp.int32))
             pick_cols[to, t * B : (t + 1) * B] = jnp.where(hit > 0, eye, 0.0).astype(BF16)
+
+
+def hand_over(*refs):
+    n = (len(refs) - 1) // 2
+    copies = [pltpu.make_async_copy(refs[i], refs[n + i], refs[-1].at[i]) for i in range(n)]
+    for copy in copies:
+        copy.start()
+    for copy in copies:
+        copy.wait()
 
 
 def on_device(
@@ -623,6 +621,7 @@
     s1, s2 = ONE * B // R, TWO * B // R
     sh = s1 + s2
     vmem = pl.BlockSpec(memory_space=pltpu.VMEM)
+    hbm = pl.BlockSpec(memory_space=pltpu.HBM)
     smem = pl.BlockSpec(memory_space=pltpu.SMEM)
     dma = pltpu.SemaphoreType.DMA
     picked = pl.pallas_call(
@@ -639,7 +638,7 @@
         compiler_params=pltpu.CompilerParams(vmem_limit_bytes=24 * 2**20),
         name="pick",
     )(blocks_one, blocks_two, inv_sep, lower_one.T, lower_two.T, upper_one, upper_two)
-    return pl.pallas_call(
+    results = pl.pallas_call(
         functools.partial(kernel, R, C, W),
         out_shape=(
             jax.ShapeDtypeStruct((s1, W), BF16),
@@ -684,6 +683,15 @@
         ),
         name="panels",
     )(*picked, corner_lower, corner_upper, diag_inv_one, diag_inv_two)
+    return pl.pallas_call(
+        hand_over,
+        out_shape=tuple(jax.ShapeDtypeStruct(a.shape, a.dtype) for a in results),
+        in_specs=[vmem] * len(results),
+        out_specs=(hbm,) * len(results),
+        scratch_shapes=[dma((len(results),))],
+        compiler_params=pltpu.CompilerParams(vmem_limit_bytes=4 * 2**20),
+        name="hand_over",
+    )(*results)
 
 
 def solution(mesh):

time: 88.7 us -> 86 us (0.970)
  local copies, waits for them, and re-layouts: 10.7 us -> 6.87 us
  Pallas kernels: 76.9 us -> 78 us
    unnamed x28 -> x22, local copies, waits for them, and re-layouts: 10.7 us -> 6.87 us
    pallas_call x0 -> x1, Pallas kernels: none -> 0.89 us  [on_device(): pl.pallas_call(hand_over, out_shape=tuple((jax.ShapeDtypeStruct(a.shape,...]
where the time goes in v4:
time: 86 us; the launch traced here: 85.6 us
  Pallas kernels  78 us (91%)
  local copies, waits for them, and re-layouts  6.87 us (8%)
    pallas_call x1, Pallas kernels, on_device(): pl.pallas_call(functools.partial(kernel, R, C, W), out_shape=(jax.ShapeDt...  74.8 us
    unnamed x22, local copies, waits for them, and re-layouts  6.87 us
    pallas_call x1, Pallas kernels, on_device(): pl.pallas_call(functools.partial(pick, R, C), out_shape=(jax.ShapeDtypeSt...  2.32 us

profile of v4, /device:TPU:1, one launch (start us, length us, event | category | flops | bytes accessed | tf_op | source)
XLA Modules:
  0.0 85.6 jit_solution(6546908713845705194)
XLA Ops:
  0.6 0.0 copy-start
  0.6 2.3 %copy-done = bf16[3072,768]{1,0:T(8,128)(2,1)S(1)} copy-done((bf16[3072,768]{1,0:T(8,128)(2,1)S(1)}, bf16[3072,768]{1,0:T(8,128)(2,1)}, u32[]{:S(2)}) %copy-start) | copy-done | bytes 4718616
  3.0 0.0 copy-start.5
  3.0 0.8 copy-done.5
  3.8 0.0 copy-start.6
  3.8 0.8 copy-done.6
  4.6 0.0 copy-start.7
  4.6 0.8 copy-done.7
  5.4 0.0 copy-start.8
  5.4 0.8 copy-done.8
  6.2 0.0 copy-start.9
  6.2 0.7 copy-done.9
  6.8 0.0 copy-start.10
  6.9 0.7 copy-done.10
  7.5 0.0 copy-start.2
  7.5 0.0 copy-start.3
  7.5 0.0 copy-start.4
  7.5 2.3 %pick.1 = (bf16[2560,640]{1,0:T(8,128)(2,1)S(1)}, bf16[2048,640]{1,0:T(8,128)(2,1)S(1)}, bf16[2,8,2560]{2,1,0:T(8,128)(2,1)S(1)}, bf16[2,32,640]{2,1,0:T(8,128)(2,1)S(1)}, bf16[640,512]{1,0:T(8,128)(2,1)S(1)}) custom-call(s32[160]{0:T(256)S(1)} %copy-done.9, s32[128]{0:T(128)S(1)} %copy-done.10, bf16[3072,768]{1,0:T(8,128)(2,1)S(1)} %copy-done, ...), custom_call_target="tpu_custom_call" | custom-call | tf_op jit(solution)/shard_map/pick/pallas_call | solution.py:627
  9.8 0.0 copy-done.1
  9.9 0.0 copy-done.2
  9.9 0.0 copy-done.3
  9.9 0.0 copy-done.4
  9.9 74.8 %panels.1 = (bf16[80,256]{1,0:T(8,128)(2,1)S(1)}, bf16[32,640]{1,0:T(8,128)(2,1)S(1)}, f32[256,256]{1,0:T(8,128)S(1)}, bf16[64,256]{1,0:T(8,128)(2,1)S(1)}, bf16...) custom-call(bf16[2560,640]{1,0:T(8,128)(2,1)S(1)} %get-tuple-element.17.sel_any, ...), custom_call_target="tpu_custom_call" | custom-call | tf_op jit(solution)/shard_map/panels/pallas_call | solution.py:641
  84.7 0.9 %hand_over.1 = (bf16[80,256]{1,0:T(8,128)(2,1)}, bf16[32,640]{1,0:T(8,128)(2,1)}, f32[256,256]{1,0:T(8,128)}, bf16[64,256]{1,0:T(8,128)(2,1)}, bf16[32,512]{1,0:T(8,128)(2,1)}, /*index=5*/f32[256,256]{1,0:T(8,128)}) custom-call(bf16[80,256]{1,0:T(8,128)(2,1)S(1)} %get-tuple-element.22.refs_0_, bf16[32,640]{1,0:T(8,128)(2,1)S(1)} %get-tuple-element.23.refs_1_, ...), custom_call_target="tpu_custom_call" | custom-call | tf_op jit(solution)/shard_map/hand_over/pallas_call | solution.py:686
  (1 shorter events, 0.0 us)
Async XLA Ops:
  0.6 2.3 %copy-start = (bf16[3072,768]{1,0:T(8,128)(2,1)S(1)}, bf16[3072,768]{1,0:T(8,128)(2,1)}, u32[]{:S(2)}) copy-start(bf16[3072,768]{1,0:T(8,128)(2,1)} %sep.1) | copy-start | bytes 14155780
  3.0 0.8 copy-start.5
  3.8 0.8 copy-start.6
  4.6 0.8 copy-start.7
  5.4 0.8 copy-start.8
  6.2 0.7 copy-start.9
  6.8 0.7 copy-start.10
  7.5 2.3 %copy-start.1 = (f32[256,256]{1,0:T(8,128)S(1)}, f32[256,256]{1,0:T(8,128)}, u32[]{:S(2)}) copy-start(f32[256,256]{1,0:T(8,128)} %dg1_ref.1) | copy-start | bytes 786436
  7.5 2.4 %copy-start.2 = (f32[256,256]{1,0:T(8,128)S(1)}, f32[256,256]{1,0:T(8,128)}, u32[]{:S(2)}) copy-start(f32[256,256]{1,0:T(8,128)} %dg2_ref.1) | copy-start | bytes 786436
  7.5 2.4 %copy-start.3 = (bf16[256,256]{1,0:T(8,128)(2,1)S(1)}, bf16[256,256]{1,0:T(8,128)(2,1)}, u32[]{:S(2)}) copy-start(bf16[256,256]{1,0:T(8,128)(2,1)} %cl_ref.1) | copy-start | bytes 393220
  7.5 2.4 %copy-start.4 = (bf16[256,256]{1,0:T(8,128)(2,1)S(1)}, bf16[256,256]{1,0:T(8,128)(2,1)}, u32[]{:S(2)}) copy-start(bf16[256,256]{1,0:T(8,128)(2,1)} %cu_ref.1) | copy-start | bytes 393220

commit v5 on v4

--- a/solution.py
+++ b/solution.py
@@ -321,8 +321,6 @@
         a_core(1 - xh, zz, k).start()
 
     loop(Z, over)
-    loop(Z // 2, lambda i: lower_at(Z // 2 + i))
-
     def rx(zz):
         return rcopy(xs.at[zz], xr.at[zz], rx_s.at[zz], rx_r.at[zz], x_dev)
 
@@ -337,6 +335,9 @@
         rx(zz).start()
 
     loop(Z, to_x)
+
+    loop(Z // 2, lambda i: lower_at(Z // 2 + i))
+
 
     def pu(j, src_r, to_r):
         return rcopy(

time: 86 us -> 85.3 us (level)
  no operation moved by 1% of the time
where the time goes in v5:
time: 85.3 us; the launch traced here: 85 us
  Pallas kernels  77.4 us (91%)
  local copies, waits for them, and re-layouts  6.87 us (8%)
    pallas_call x1, Pallas kernels, on_device(): pl.pallas_call(functools.partial(kernel, R, C, W), out_shape=(jax.ShapeDt...  74.2 us
    unnamed x22, local copies, waits for them, and re-layouts  6.87 us
    pallas_call x1, Pallas kernels, on_device(): pl.pallas_call(functools.partial(pick, R, C), out_shape=(jax.ShapeDtypeSt...  2.32 us

profile of v5, /device:TPU:1, one launch (start us, length us, event | category | flops | bytes accessed | tf_op | source)
XLA Modules:
  0.0 85.0 jit_solution(1042923452257420551)
XLA Ops:
  0.6 0.0 copy-start
  0.6 2.3 %copy-done = bf16[3072,768]{1,0:T(8,128)(2,1)S(1)} copy-done((bf16[3072,768]{1,0:T(8,128)(2,1)S(1)}, bf16[3072,768]{1,0:T(8,128)(2,1)}, u32[]{:S(2)}) %copy-start) | copy-done | bytes 4718616
  3.0 0.0 copy-start.5
  3.0 0.8 copy-done.5
  3.8 0.8 copy-done.6
  4.6 0.0 copy-start.7
  4.6 0.8 copy-done.7
  5.4 0.0 copy-start.8
  5.4 0.8 copy-done.8
  6.2 0.0 copy-start.9
  6.2 0.7 copy-done.9
  6.8 0.0 copy-start.10
  6.9 0.7 copy-done.10
  7.5 0.0 copy-start.1
  7.5 0.0 copy-start.2
  7.5 0.0 copy-start.3
  7.5 0.0 copy-start.4
  7.5 2.3 %pick.1 = (bf16[2560,640]{1,0:T(8,128)(2,1)S(1)}, bf16[2048,640]{1,0:T(8,128)(2,1)S(1)}, bf16[2,8,2560]{2,1,0:T(8,128)(2,1)S(1)}, bf16[2,32,640]{2,1,0:T(8,128)(2,1)S(1)}, bf16[640,512]{1,0:T(8,128)(2,1)S(1)}) custom-call(s32[160]{0:T(256)S(1)} %copy-done.9, s32[128]{0:T(128)S(1)} %copy-done.10, bf16[3072,768]{1,0:T(8,128)(2,1)S(1)} %copy-done, ...), custom_call_target="tpu_custom_call" | custom-call | tf_op jit(solution)/shard_map/pick/pallas_call | solution.py:628
  9.8 0.0 copy-done.1
  9.9 0.0 copy-done.2
  9.9 0.0 copy-done.3
  9.9 0.0 copy-done.4
  9.9 74.2 %panels.1 = (bf16[80,256]{1,0:T(8,128)(2,1)S(1)}, bf16[32,640]{1,0:T(8,128)(2,1)S(1)}, f32[256,256]{1,0:T(8,128)S(1)}, bf16[64,256]{1,0:T(8,128)(2,1)S(1)}, bf16...) custom-call(bf16[2560,640]{1,0:T(8,128)(2,1)S(1)} %get-tuple-element.17.sel_any, ...), custom_call_target="tpu_custom_call" | custom-call | tf_op jit(solution)/shard_map/panels/pallas_call | solution.py:642
  84.1 0.9 %hand_over.1 = (bf16[80,256]{1,0:T(8,128)(2,1)}, bf16[32,640]{1,0:T(8,128)(2,1)}, f32[256,256]{1,0:T(8,128)}, bf16[64,256]{1,0:T(8,128)(2,1)}, bf16[32,512]{1,0:T(8,128)(2,1)}, /*index=5*/f32[256,256]{1,0:T(8,128)}) custom-call(bf16[80,256]{1,0:T(8,128)(2,1)S(1)} %get-tuple-element.22.refs_0_, bf16[32,640]{1,0:T(8,128)(2,1)S(1)} %get-tuple-element.23.refs_1_, ...), custom_call_target="tpu_custom_call" | custom-call | tf_op jit(solution)/shard_map/hand_over/pallas_call | solution.py:687
  (1 shorter events, 0.0 us)
Async XLA Ops:
  0.6 2.3 %copy-start = (bf16[3072,768]{1,0:T(8,128)(2,1)S(1)}, bf16[3072,768]{1,0:T(8,128)(2,1)}, u32[]{:S(2)}) copy-start(bf16[3072,768]{1,0:T(8,128)(2,1)} %sep.1) | copy-start | bytes 14155780
  3.0 0.8 copy-start.5
  3.8 0.8 copy-start.6
  4.6 0.8 copy-start.7
  5.4 0.8 copy-start.8
  6.2 0.7 copy-start.9
  6.8 0.7 copy-start.10
  7.5 2.3 %copy-start.1 = (f32[256,256]{1,0:T(8,128)S(1)}, f32[256,256]{1,0:T(8,128)}, u32[]{:S(2)}) copy-start(f32[256,256]{1,0:T(8,128)} %dg1_ref.1) | copy-start | bytes 786436
  7.5 2.4 %copy-start.2 = (f32[256,256]{1,0:T(8,128)S(1)}, f32[256,256]{1,0:T(8,128)}, u32[]{:S(2)}) copy-start(f32[256,256]{1,0:T(8,128)} %dg2_ref.1) | copy-start | bytes 786436
  7.5 2.4 %copy-start.3 = (bf16[256,256]{1,0:T(8,128)(2,1)S(1)}, bf16[256,256]{1,0:T(8,128)(2,1)}, u32[]{:S(2)}) copy-start(bf16[256,256]{1,0:T(8,128)(2,1)} %cl_ref.1) | copy-start | bytes 393220
  7.5 2.4 %copy-start.4 = (bf16[256,256]{1,0:T(8,128)(2,1)S(1)}, bf16[256,256]{1,0:T(8,128)(2,1)}, u32[]{:S(2)}) copy-start(bf16[256,256]{1,0:T(8,128)(2,1)} %cu_ref.1) | copy-start | bytes 393220
